TPU v7x, 32 devices: a whole 2x2x4 slice. The times are simulated.
32 devices in a mesh: ep: 8 (over z, x), tp: 4 (over y, core).
Axes of the slice: x: 2, y: 2, z: 4, core: 2. Of those that a mesh axis runs over, the one named last changes fastest.
Arguments:
- tokens: bfloat16 [6144, 2048], P('ep'), may hold values from -6 to 6
- lengths: int32 [8], P('ep'), may hold values from 384 to 768, as said below
- routes: int32 [6144, 4], P('ep'), may hold values from 0 to 7, all different within a row
- route_weights: float32 [6144, 4], P('ep'), may hold values from 0.1 to 0.6
- slot_order: int32 [8, 768], P('ep'), may hold values from 0 to 767, each once within a row
- norm_one_gain: bfloat16 [2048], P('ep'), may hold values from 0.5 to 1.5
- query_weight: bfloat16 [2048, 2048], P('ep', 'tp'), may hold values from -0.125 to 0.125
- key_weight: bfloat16 [2048, 2048], P('ep', 'tp'), may hold values from -0.125 to 0.125
- value_weight: bfloat16 [2048, 2048], P('ep', 'tp'), may hold values from -0.125 to 0.125
- query_bias: bfloat16 [16, 128], P('tp', 'ep'), may hold values from -3 to 3
- key_bias: bfloat16 [16, 128], P('tp', 'ep'), may hold values from -3 to 3
- value_bias: bfloat16 [16, 128], P('tp', 'ep'), may hold values from -3 to 3
- output_weight: bfloat16 [2048, 2048], P('tp', 'ep'), may hold values from -0.5 to 0.5
- norm_two_gain: bfloat16 [2048], P('ep'), may hold values from 0.5 to 1.5
- shared_gate: bfloat16 [2048, 5632], P('ep', 'tp'), may hold values from -0.125 to 0.125
- shared_up: bfloat16 [2048, 5632], P('ep', 'tp'), may hold values from -0.125 to 0.125
- shared_down: bfloat16 [5632, 2048], P('tp', 'ep'), may hold values from -0.078125 to 0.078125
- shared_switch: bfloat16 [2048], P('ep'), may hold values from -0.125 to 0.125
- expert_gate: bfloat16 [8, 2048, 1408], P('ep', None, 'tp'), may hold values from -0.125 to 0.125
- expert_up: bfloat16 [8, 2048, 1408], P('ep', None, 'tp'), may hold values from -0.125 to 0.125
- expert_down: bfloat16 [8, 1408, 2048], P('ep', 'tp'), may hold values from -0.15625 to 0.15625
- cotangent: bfloat16 [6144, 2048], P('ep'), may hold values from -6 to 6
Outputs:
- output: bfloat16 [6144, 2048], P('ep')
- grad_tokens: bfloat16 [6144, 2048], P('ep')
- grad_norm_one_gain: float32 [2048], P('ep')
- grad_query_weight: float32 [2048, 2048], P('ep', 'tp')
- grad_key_weight: float32 [2048, 2048], P('ep', 'tp')
- grad_value_weight: float32 [2048, 2048], P('ep', 'tp')
- grad_query_bias: float32 [16, 128], P('tp', 'ep')
- grad_key_bias: float32 [16, 128], P('tp', 'ep')
- grad_value_bias: float32 [16, 128], P('tp', 'ep')
- grad_output_weight: float32 [2048, 2048], P('tp', 'ep')
- grad_norm_two_gain: float32 [2048], P('ep')
- grad_shared_gate: float32 [2048, 5632], P('ep', 'tp')
- grad_shared_up: float32 [2048, 5632], P('ep', 'tp')
- grad_shared_down: float32 [5632, 2048], P('tp', 'ep')
- grad_shared_switch: float32 [2048], P('ep')
- grad_expert_gate: float32 [8, 2048, 1408], P('ep', None, 'tp')
- grad_expert_up: float32 [8, 2048, 1408], P('ep', None, 'tp')
- grad_expert_down: float32 [8, 1408, 2048], P('ep', 'tp')
Inputs may be any that keep to these rules, and one draw needn't show every extreme that they name: `lengths`: each block's sequence has at least 384 tokens; some block is filled by its sequence in every draw. `routes`: each row names 4 different experts; every expert is named by some row. `slot_order`: each block's row is a permutation of 0 to 767.
All inputs are finite; a program needn't handle non-finite values.
Results may differ from a plain program's by a relative error of at most 0.028.
Values may be sent and summed in bfloat16 or wider, within the bound.
No kernel may reach another device: no remote copies, remote signals or barrier semaphores. Data moves between devices by JAX's collectives and lax.ppermute only.
A program may use at most 320 MiB of HBM per device.

v0:
```python
import jax
import jax.numpy as jnp
from jax import lax
from jax.sharding import PartitionSpec as P


norm_eps = 1e-06
rope_base = 1000000.0


def rms_factor(values):
    return lax.rsqrt(jnp.mean(values * values, axis=-1, keepdims=True) + norm_eps)


def rotary_tables(row_count, head_size):
    half_size = head_size // 2
    inverse = rope_base ** (-(jnp.arange(half_size, dtype=jnp.float32) * 2.0 / head_size))
    angles = jnp.arange(row_count, dtype=jnp.float32)[:, None] * inverse[None, :]
    cosine = jnp.concatenate([jnp.cos(angles), jnp.cos(angles)], axis=1)
    sine = jnp.concatenate([jnp.sin(angles), jnp.sin(angles)], axis=1)
    return (cosine[None], sine[None])


def rotate_forward(values, cosine, sine):
    half_size = values.shape[-1] // 2
    turned = jnp.concatenate([-values[..., half_size:], values[..., :half_size]], axis=-1)
    return values * cosine + turned * sine


def rotate_backward(grads, cosine, sine):
    half_size = grads.shape[-1] // 2
    scaled = grads * sine
    turned = jnp.concatenate([scaled[..., half_size:], -scaled[..., :half_size]], axis=-1)
    return grads * cosine + turned


def by_head(values, heads):
    size = values.shape[1] // heads
    return jnp.stack([values[:, h * size : (h + 1) * size] for h in range(heads)])


def side_by_side(values):
    return jnp.concatenate([values[h] for h in range(values.shape[0])], axis=1)


def times(left, right):
    return jnp.dot(left, right, preferred_element_type=jnp.float32)


def contract_rows(left, right):
    return lax.dot_general(
        left, right, (((0,), (0,)), ((), ())), preferred_element_type=jnp.float32
    )


def times_transpose(left, right):
    return lax.dot_general(
        left, right, (((1,), (1,)), ((), ())), preferred_element_type=jnp.float32
    )


def low(values):
    return values.astype(jnp.bfloat16)


def masked_scores(queries, keys, length_now, score_scale):
    scores = (
        jnp.einsum("htd,hsd->hts", queries, keys, preferred_element_type=jnp.float32) * score_scale
    )
    row_count = queries.shape[1]
    rows_at = jnp.arange(row_count)[:, None]
    cols_at = jnp.arange(row_count)[None, :]
    allowed = (cols_at <= rows_at) & (cols_at < length_now)
    return jnp.where(allowed[None], scores, -1e30)


def slot_plan(route_rows, rank_rows, valid_rows, experts_total, capacity):
    experts = jnp.arange(experts_total, dtype=jnp.int32)
    chosen = jnp.any(route_rows[:, :, None] == experts[None, None, :], axis=1)
    chosen = low(chosen & valid_rows[:, None])
    earlier = low(rank_rows[None, :] < rank_rows[:, None])
    counts = times(earlier, chosen).astype(jnp.int32)
    mine = route_rows[:, :, None] == experts[None, None, :]
    slots = jnp.sum(jnp.where(mine, counts[:, None, :], 0), axis=2)
    kept = valid_rows[:, None] & (slots < capacity)
    return (kept, slots)


def ring_order(count):
    return [*range(0, count, 2), *range(count - 1, 0, -2)]


def take_blocks(values, order, axis):
    size = values.shape[axis] // len(order)
    return jnp.concatenate(
        [lax.slice_in_dim(values, i * size, (i + 1) * size, axis=axis) for i in order], axis=axis
    )


def to_ring(values, axis):
    return take_blocks(values, ring_order(lax.axis_size("ep")), axis)


def from_ring(values, axis):
    order = ring_order(lax.axis_size("ep"))
    return take_blocks(values, [order.index(i) for i in range(len(order))], axis)


def ring_gather(shard):
    return lax.all_gather(
        shard, "ep", axis=0, tiled=True, axis_index_groups=[ring_order(lax.axis_size("ep"))]
    )


def ring_scatter(full):
    return lax.psum_scatter(
        full,
        "ep",
        scatter_dimension=0,
        tiled=True,
        axis_index_groups=[ring_order(lax.axis_size("ep"))],
    )


def after(values, *tokens):
    return lax.optimization_barrier((values, *tokens))[0]


def pair_up(values, distance):
    count = lax.axis_size("ep")
    return lax.ppermute(values, "ep", [(i, i ^ distance) for i in range(count)])


def small_gather(row):
    count = lax.axis_size("ep")
    index = lax.axis_index("ep")
    zero = jnp.zeros_like(index)
    full = jnp.broadcast_to(row[None], (count, row.shape[0]))
    distance = 1
    while distance < count:
        start = lax.div(index, distance) * distance
        other = start + distance - 2 * lax.rem(start, 2 * distance)
        block = lax.dynamic_slice(full, (start, zero), (distance, row.shape[0]))
        full = lax.dynamic_update_slice(full, pair_up(block, distance), (other, zero))
        distance *= 2
    return full


def small_scatter(rows):
    index = lax.axis_index("ep")
    distance = lax.axis_size("ep") // 2
    while distance >= 1:
        mine = lax.rem(lax.div(index, distance), 2)
        halves = rows.reshape(2, distance, rows.shape[1])
        kept = lax.dynamic_index_in_dim(halves, mine, 0, keepdims=False)
        sent = lax.dynamic_index_in_dim(halves, 1 - mine, 0, keepdims=False)
        rows = kept + pair_up(sent, distance)
        distance //= 2
    return rows[0]


def inner(values):
    return lax.ppermute(values, "tp", [(i, i ^ 1) for i in range(4)])


def outer(values):
    return lax.ppermute(values, "tp", [(i, i ^ 2) for i in range(4)])


def tp_place():
    member = lax.axis_index("tp")
    return lax.div(member, 2), lax.rem(member, 2)


def rows_scatter(partial):
    outer_at, inner_at = tp_place()
    rows, width = partial.shape
    split = partial.reshape(2, 2, rows // 4, width)
    arrived = inner(lax.dynamic_index_in_dim(split, 1 - inner_at, 1, keepdims=False))
    mine = lax.dynamic_index_in_dim(split, inner_at, 1, keepdims=False)
    summed = mine.astype(jnp.float32) + arrived.astype(jnp.float32)
    sent = low(lax.dynamic_index_in_dim(summed, 1 - outer_at, 0, keepdims=False))
    kept = lax.dynamic_index_in_dim(summed, outer_at, 0, keepdims=False)
    arrived = outer(sent)
    return kept + arrived.astype(jnp.float32), sent


def rows_gather(rows):
    outer_at, inner_at = tp_place()
    count, width = rows.shape
    across = outer(rows)
    beside = inner(rows)
    diagonal = inner(across)
    full = jnp.zeros((4 * count, width), rows.dtype)

    def put(full, piece, outer_now, inner_now):
        at = (outer_now * 2 + inner_now) * count
        return lax.dynamic_update_slice(full, piece, (at, jnp.zeros_like(at)))

    full = put(full, rows, outer_at, inner_at)
    full = put(full, beside, outer_at, 1 - inner_at)
    full = put(full, across, 1 - outer_at, inner_at)
    return put(full, diagonal, 1 - outer_at, 1 - inner_at)


def tp_pieces(own):
    across = outer(own)
    beside = inner(own)
    return [own, beside, across, inner(across)]


def tp_reduce(pieces):
    own, beside, across, diagonal = pieces
    near = inner(beside)
    sent = low(across.astype(jnp.float32) + inner(diagonal).astype(jnp.float32))
    far = outer(sent)
    return (own, near, far), sent


def add_terms(terms):
    own, near, far = (term.astype(jnp.float32) for term in terms)
    return own + near + far


def tp_sum(values):
    values = values + inner(values)
    return values + outer(values)


def exchange(rows):
    return lax.all_to_all(rows, "ep", split_axis=0, concat_axis=0, tiled=True)


def body(
    tokens,
    lengths,
    routes,
    route_weights,
    slot_order,
    norm_one_gain,
    query_weight,
    key_weight,
    value_weight,
    query_bias,
    key_bias,
    value_bias,
    output_weight,
    norm_two_gain,
    shared_gate,
    shared_up,
    shared_down,
    shared_switch,
    expert_gate,
    expert_up,
    expert_down,
    cotangent,
):
    ep_count = lax.axis_size("ep")
    row_count, model_width = tokens.shape
    heads_here, bias_part = query_bias.shape
    head_size = bias_part * ep_count
    heads_width = heads_here * head_size
    shared_hidden = shared_gate.shape[1]
    expert_hidden = expert_gate.shape[2]
    gain_part = norm_one_gain.shape[0]
    tp_at = lax.axis_index("tp")
    own_count = row_count // 4
    own_start = tp_at * own_count

    def own_rows(values):
        return lax.dynamic_slice_in_dim(values, own_start, own_count, 0)

    small = jnp.concatenate(
        [
            norm_one_gain,
            norm_two_gain,
            shared_switch,
            query_bias.reshape(-1),
            key_bias.reshape(-1),
            value_bias.reshape(-1),
        ]
    )
    full_qkv = ring_gather(jnp.concatenate([query_weight, key_weight, value_weight], axis=1))
    output_turned = output_weight.T
    shared_in = jnp.concatenate([shared_gate, shared_up], axis=1)
    shared_out = shared_down.T
    full_output = ring_gather(output_turned)
    full_shared = ring_gather(shared_in)
    full_down = ring_gather(shared_out)
    small = to_ring(small_gather(small), 0)
    gain_one = small[:, :gain_part].reshape(-1).astype(jnp.float32)
    gain_two = small[:, gain_part : 2 * gain_part].reshape(-1).astype(jnp.float32)
    full_switch = small[:, 2 * gain_part : 3 * gain_part].reshape(-1)
    bias_all = (
        from_ring(small[:, 3 * gain_part :], 0)
        .reshape(ep_count, 3 * heads_here, bias_part)
        .transpose(1, 0, 2)
        .reshape(-1)
        .astype(jnp.float32)
    )

    group = -(-expert_hidden // 128) * 128
    spare = group - expert_hidden

    def padded(weight):
        return jnp.pad(weight, ((0, 0), (0, spare)))

    expert_own = jnp.concatenate([padded(expert_gate[0]), padded(expert_up[0])], axis=1)
    expert_own = to_ring(expert_own, 0)
    expert_last = to_ring(expert_down[0], 1)
    expert_in = jnp.concatenate(tp_pieces(expert_own), axis=1)
    expert_out = jnp.zeros((4 * group, model_width), jnp.bfloat16)
    for i, piece in enumerate(tp_pieces(expert_last)):
        expert_out = lax.dynamic_update_slice(expert_out, piece, (i * group, 0))

    def gate_columns(values):
        return [values[:, (2 * i) * group : (2 * i + 1) * group] for i in range(4)]

    def up_columns(values):
        return [values[:, (2 * i + 1) * group : (2 * i + 2) * group] for i in range(4)]

    score_scale = head_size ** (-0.5)
    length_now = lengths[0]
    valid_rows = jnp.arange(row_count) < length_now
    valid_float = valid_rows.astype(jnp.float32)[:, None]
    experts_total = ep_count
    top_count = routes.shape[1]
    capacity = row_count * top_count // experts_total
    slots_here = capacity // 4
    slot_rows = experts_total * slots_here
    kept, slots = slot_plan(routes, slot_order[0], valid_rows, experts_total, capacity)
    slots = slots - tp_at * slots_here
    taken = kept & (slots >= 0) & (slots < slots_here)
    target = jnp.where(taken, routes * slots_here + slots, -1)
    slot_ids = jnp.arange(slot_rows, dtype=jnp.int32)[:, None]
    select = jnp.zeros((slot_rows, row_count), jnp.float32)
    weighted = jnp.zeros((slot_rows, row_count), jnp.float32)
    for choice in range(top_count):
        hit = slot_ids == target[:, choice][None, :]
        select = jnp.where(hit, 1.0, select)
        weighted = jnp.where(hit, route_weights[:, choice][None, :], weighted)
    select, weighted = low(select), low(weighted)

    grad_low = to_ring(cotangent, 1)
    grad_low = jnp.where(valid_rows[:, None], grad_low, jnp.zeros_like(grad_low))
    grad_out = grad_low.astype(jnp.float32)
    grad_sent = low(times(weighted, grad_low))
    grad_sent = grad_sent.reshape(experts_total, slots_here, model_width)
    grad_arrived = exchange(after(grad_sent, full_qkv))
    grad_arrived = grad_arrived.reshape(slot_rows, model_width)

    tokens = to_ring(tokens, 1)
    inputs = tokens.astype(jnp.float32)
    factor_one = rms_factor(inputs)
    cosine, sine = rotary_tables(row_count, head_size)
    normed_one = low(inputs * factor_one * gain_one)
    qkv = times(normed_one, full_qkv) + bias_all
    query_pre, key_pre, value_pre = (
        by_head(qkv[:, i * heads_width : (i + 1) * heads_width], heads_here)
        for i in range(3)
    )
    queries = low(rotate_forward(query_pre, cosine, sine))
    keys_rot = low(rotate_forward(key_pre, cosine, sine))
    values = low(value_pre)
    scores = masked_scores(queries, keys_rot, length_now, score_scale)
    peak = jnp.max(scores, axis=-1, keepdims=True)
    raised = jnp.exp(scores - peak)
    totals = jnp.sum(raised, axis=-1, keepdims=True)
    probs = raised / totals
    log_total = peak + jnp.log(totals)
    attended = jnp.einsum("hts,hsd->htd", low(probs), values, preferred_element_type=jnp.float32)
    attended_low = low(side_by_side(attended))
    attn_part = low(times_transpose(attended_low, full_output))
    own_inputs = own_rows(tokens).astype(jnp.float32)
    hidden = own_inputs + rows_scatter(attn_part)[0]
    factor_two = rms_factor(hidden)
    own_normed_two = low(hidden * factor_two * gain_two)
    normed_two = rows_gather(own_normed_two)

    sent = low(times(select, normed_two)).reshape(experts_total, slots_here, model_width)
    arrived = exchange(after(sent, grad_arrived)).reshape(slot_rows, model_width)
    act = times(arrived, expert_in)
    gate_act = jnp.concatenate(gate_columns(act), axis=1)
    up_act = jnp.concatenate(up_columns(act), axis=1)
    sigma = jax.nn.sigmoid(gate_act)
    swish = gate_act * sigma
    inner_act = low(swish * up_act)
    inner_grad = times_transpose(grad_arrived, expert_out)
    up_grad = low(inner_grad * swish)
    gate_grad = low(inner_grad * up_act * sigma * (1.0 + gate_act * (1.0 - sigma)))
    both_grad = jnp.concatenate(
        [part[:, i * group : (i + 1) * group] for i in range(4) for part in (gate_grad, up_grad)],
        axis=1,
    )
    back_rows = low(times_transpose(both_grad, expert_in))
    back_home = exchange(back_rows.reshape(experts_total, slots_here, model_width))
    back_home = back_home.reshape(slot_rows, model_width)
    both_last, inner_last = after((both_grad, inner_act), back_rows)
    grad_in = low(contract_rows(arrived, both_last))
    grad_in_terms, grad_in_sent = tp_reduce(
        [grad_in[:, 2 * i * group : 2 * (i + 1) * group] for i in range(4)]
    )
    inner_last = after(inner_last, grad_in)
    grad_down = low(contract_rows(inner_last, grad_arrived))
    grad_down_near = inner(
        jnp.stack([grad_down[i * group : i * group + expert_hidden] for i in (1, 3)])
    )
    produced = low(times(after(inner_last, grad_down), expert_out))
    produced_home = exchange(
        after(produced, back_home).reshape(experts_total, slots_here, model_width)
    )
    produced_home = produced_home.reshape(slot_rows, model_width)

    shared_rows = after(normed_two, produced, grad_in_sent)
    shared_act = times(shared_rows, full_shared)
    shared_gate_act = shared_act[:, :shared_hidden]
    shared_up_act = shared_act[:, shared_hidden:]
    shared_sigma = jax.nn.sigmoid(shared_gate_act)
    shared_swish = shared_gate_act * shared_sigma
    shared_inner = low(shared_swish * shared_up_act)
    switch_value = jax.nn.sigmoid(
        jnp.sum(shared_rows.astype(jnp.float32) * full_switch.astype(jnp.float32), axis=1)
    )
    shared_out_grad = low(switch_value[:, None] * grad_out)
    shared_inner_grad = times(shared_out_grad, full_down)
    shared_up_grad = low(shared_inner_grad * shared_swish)
    shared_gate_grad = low(
        shared_inner_grad
        * shared_up_act
        * shared_sigma
        * (1.0 + shared_gate_act * (1.0 - shared_sigma))
    )
    shared_grad = jnp.concatenate([shared_gate_grad, shared_up_grad], axis=1)
    shared_part_grad = low(contract_rows(shared_rows, shared_grad))
    grad_shared = ring_scatter(shared_part_grad)
    grad_shared_gate = grad_shared[:, :shared_hidden].astype(jnp.float32)
    grad_shared_up = grad_shared[:, shared_hidden:].astype(jnp.float32)
    shared_grad, select_then = after((shared_grad, select), shared_part_grad)
    normed_two_part = times_transpose(shared_grad, full_shared)
    normed_two_part = normed_two_part + contract_rows(select_then, back_home)
    normed_two_grad, normed_two_sent = rows_scatter(low(normed_two_part))
    shared_inner, shared_out_grad = after((shared_inner, shared_out_grad), normed_two_sent)
    shared_part = times_transpose(shared_inner, full_down)
    switch_total = jnp.sum(grad_out * shared_part, axis=1).reshape(-1, 128)
    switch_total = tp_sum(switch_total).reshape(-1)
    logit_grad = switch_total * switch_value * (1.0 - switch_value)

    own_logit_grad = own_rows(logit_grad)[:, None]
    normed_two_grad = normed_two_grad + own_logit_grad * full_switch.astype(jnp.float32)[None, :]
    switch_gradient = jnp.sum(own_logit_grad * own_normed_two.astype(jnp.float32), axis=0)
    second_gain_gradient = jnp.sum(normed_two_grad * hidden * factor_two, axis=0)
    scaled_two = normed_two_grad * gain_two
    hidden_grad = (
        own_rows(grad_out)
        + factor_two * scaled_two
        - hidden * factor_two**3 * jnp.mean(scaled_two * hidden, axis=-1, keepdims=True)
    )
    own_attn_grad = low(hidden_grad)
    attn_grad_low = rows_gather(own_attn_grad)

    grad_down, grad_down_near = after((grad_down, grad_down_near), attn_grad_low)
    grad_down_parts = [grad_down[i * group : i * group + expert_hidden] for i in (0, 2)]
    grad_down_far = outer(
        low(grad_down_parts[1].astype(jnp.float32) + grad_down_near[1].astype(jnp.float32))
    )
    grad_down_terms = (grad_down_parts[0], grad_down_near[0], grad_down_far)
    shared_out_grad = after(shared_out_grad, own_attn_grad)
    shared_down_part = low(contract_rows(shared_out_grad, shared_inner))
    grad_shared_down = ring_scatter(shared_down_part).T.astype(jnp.float32)
    attn_grad_low = after(attn_grad_low, shared_down_part)
    attended_flat = low(times(attn_grad_low, full_output))
    attended_grad = by_head(attended_flat, heads_here)
    scores_again = masked_scores(queries, keys_rot, length_now, score_scale)
    probs_again = jnp.exp(scores_again - log_total)
    value_grad = jnp.einsum(
        "hts,htd->hsd", low(probs_again), attended_grad, preferred_element_type=jnp.float32
    )
    probs_grad = jnp.einsum(
        "htd,hsd->hts", attended_grad, values, preferred_element_type=jnp.float32
    )
    row_dot = jnp.sum(probs_again * probs_grad, axis=-1, keepdims=True)
    score_grad = low(probs_again * (probs_grad - row_dot))
    query_grad = (
        jnp.einsum("hts,hsd->htd", score_grad, keys_rot, preferred_element_type=jnp.float32)
        * score_scale
    )
    key_grad = (
        jnp.einsum("hts,htd->hsd", score_grad, queries, preferred_element_type=jnp.float32)
        * score_scale
    )
    query_pre_grad = low(side_by_side(rotate_backward(query_grad, cosine, sine)))
    key_pre_grad = low(side_by_side(rotate_backward(key_grad, cosine, sine)))
    value_pre_grad = low(side_by_side(value_grad))
    qkv_grad = jnp.concatenate([query_pre_grad, key_pre_grad, value_pre_grad], axis=1)
    bias_grad = jnp.sum(qkv_grad.astype(jnp.float32), axis=0)
    mixed = contract_rows(weighted, produced_home) + switch_value[:, None] * shared_part
    mixed = after(low(mixed), attended_flat)
    own_valid = own_rows(valid_float)
    output = rows_gather(from_ring(low(own_valid * (hidden + rows_scatter(mixed)[0])), 1))

    qkv_part = contract_rows(normed_one, qkv_grad)
    qkv_grad = after(qkv_grad, qkv_part)
    normed_one_grad, _ = rows_scatter(low(times_transpose(qkv_grad, full_qkv)))
    grad_in_terms, grad_down_terms = after((grad_in_terms, grad_down_terms), qkv_part)
    grad_expert_gate = from_ring(add_terms([t[:, :expert_hidden] for t in grad_in_terms]), 0)[None]
    grad_expert_up = from_ring(
        add_terms([t[:, group : group + expert_hidden] for t in grad_in_terms]), 0
    )[None]
    grad_expert_down = from_ring(add_terms(grad_down_terms), 1)[None]
    own_factor = own_rows(factor_one)
    first_gain_gradient = jnp.sum(normed_one_grad * own_inputs * own_factor, axis=0)
    scaled_one = normed_one_grad * gain_one
    token_gradient = (
        hidden_grad
        + own_factor * scaled_one
        - own_inputs * own_factor**3 * jnp.mean(scaled_one * own_inputs, axis=-1, keepdims=True)
    )
    own_token_gradient = from_ring(low(token_gradient), 1)
    token_gradient = rows_gather(own_token_gradient)
    grad_qkv = ring_scatter(
        jnp.concatenate(
            [low(qkv_part), low(contract_rows(attn_grad_low, attended_low))], axis=1
        ),
    ).astype(jnp.float32)
    grad_output_weight = grad_qkv[:, 3 * heads_width :].T
    grad_query_weight, grad_key_weight, grad_value_weight = (
        grad_qkv[:, i * heads_width : (i + 1) * heads_width] for i in range(3)
    )

    row_sums = tp_sum(jnp.stack([first_gain_gradient, second_gain_gradient, switch_gradient]))
    small_grad = jnp.concatenate(
        [
            from_ring(
                row_sums.reshape(3, ep_count, gain_part).transpose(1, 0, 2).reshape(ep_count, -1),
                0,
            ),
            bias_grad.reshape(3 * heads_here, ep_count, bias_part)
            .transpose(1, 0, 2)
            .reshape(ep_count, -1),
        ],
        axis=1,
    )
    small_grad = small_scatter(small_grad)
    first_gain_gradient, second_gain_gradient, switch_gradient = (
        small_grad[i * gain_part : (i + 1) * gain_part] for i in range(3)
    )
    bias_size = heads_here * bias_part
    grad_query_bias, grad_key_bias, grad_value_bias = (
        small_grad[3 * gain_part + i * bias_size : 3 * gain_part + (i + 1) * bias_size].reshape(
            heads_here, bias_part
        )
        for i in range(3)
    )
    return (
        output,
        token_gradient,
        first_gain_gradient,
        grad_query_weight,
        grad_key_weight,
        grad_value_weight,
        grad_query_bias,
        grad_key_bias,
        grad_value_bias,
        grad_output_weight,
        second_gain_gradient,
        grad_shared_gate,
        grad_shared_up,
        grad_shared_down,
        switch_gradient,
        grad_expert_gate,
        grad_expert_up,
        grad_expert_down,
    )


def solution(mesh):
    in_specs = (
        P("ep", None),
        P("ep"),
        P("ep", None),
        P("ep", None),
        P("ep", None),
        P("ep"),
        P("ep", "tp"),
        P("ep", "tp"),
        P("ep", "tp"),
        P("tp", "ep"),
        P("tp", "ep"),
        P("tp", "ep"),
        P("tp", "ep"),
        P("ep"),
        P("ep", "tp"),
        P("ep", "tp"),
        P("tp", "ep"),
        P("ep"),
        P("ep", None, "tp"),
        P("ep", None, "tp"),
        P("ep", "tp", None),
        P("ep", None),
    )
    out_specs = (
        P("ep", None),
        P("ep", None),
        P("ep"),
        P("ep", "tp"),
        P("ep", "tp"),
        P("ep", "tp"),
        P("tp", "ep"),
        P("tp", "ep"),
        P("tp", "ep"),
        P("tp", "ep"),
        P("ep"),
        P("ep", "tp"),
        P("ep", "tp"),
        P("tp", "ep"),
        P("ep"),
        P("ep", None, "tp"),
        P("ep", None, "tp"),
        P("ep", "tp", None),
    )

    return jax.shard_map(body, mesh=mesh, in_specs=in_specs, out_specs=out_specs, check_vma=False)
```

profile of v0, /device:TPU:0, one launch (start us, length us, event | category | flops | bytes accessed | tf_op | source)
XLA Modules:
  0.0 931.3 jit_solution(18280717030589713992)
XLA Ops:
  60.2 20.5 %all-gather.5.cloned.1.call-done = bf16[2048,1536]{1,0:T(8,128)(2,1)} async-done(((bf16[256,1536]{1,0:T(8,128)(2,1)}), bf16[2048,1536]{1,0:T(8,128)(2,1)}) %all-gather.5.cloned.1.call-update) | async-done | bytes 6291472 | tf_op jit(solution)/shard_map/all_gather | solution.py:110
  102.2 20.5 %all-gather.7.cloned.1.call-done = bf16[2048,512]{0,1:T(8,128)(2,1)} async-done(((bf16[256,512]{0,1:T(8,128)(2,1)}), bf16[2048,512]{0,1:T(8,128)(2,1)}) %all-gather.7.cloned.1.call-update) | async-done | bytes 2097168 | tf_op jit(solution)/shard_map/all_gather | solution.py:110
  148.4 16.0 %collective-permute-done.4 = bf16[192,2048]{1,0:T(8,128)(2,1)} collective-permute-done((bf16[192,2048]{1,0:T(8,128)(2,1)}, bf16[192,2048]{1,0:T(8,128)(2,1)}, u32[]{:S(2)}, u32[]{:S(2)}) %collective-permute-start.4) | collective-permute-done | bytes 786464 | tf_op jit(solution)/shard_map/ppermute | solution.py:167
  173.2 14.5 %collective-permute-done.9 = bf16[192,2048]{1,0:T(8,128)(2,1)} collective-permute-done((bf16[192,2048]{1,0:T(8,128)(2,1)}, bf16[192,2048]{1,0:T(8,128)(2,1)}, u32[]{:S(2)}, u32[]{:S(2)}) %collective-permute-start.9) | collective-permute-done | bytes 786464 | tf_op jit(solution)/shard_map/ppermute | solution.py:167
  198.9 46.5 %all-to-all-done = bf16[8,96,2048]{2,1,0:T(8,128)(2,1)} async-done(((bf16[8,96,2048]{2,1,0:T(8,128)(2,1)}), bf16[8,96,2048]{2,1,0:T(8,128)(2,1)}, u32[]{:S(2)}, u32[]{:S(2)}) %all-to-all-start) | async-done | bytes 3145760 | tf_op jit(solution)/shard_map/all_to_all | solution.py:231
  263.5 32.6 %collective-permute-done.6 = bf16[352,2048]{1,0:T(8,128)(2,1)} collective-permute-done((bf16[352,2048]{1,0:T(8,128)(2,1)}, bf16[352,2048]{1,0:T(8,128)(2,1)}, u32[]{:S(2)}, u32[]{:S(2)}) %collective-permute-start.6) | collective-permute-done | bytes 1441824 | tf_op jit(solution)/shard_map/ppermute | solution.py:167
  309.0 46.2 %all-to-all-done.1 = bf16[8,96,2048]{2,1,0:T(8,128)(2,1)S(1)} async-done(((bf16[8,96,2048]{2,1,0:T(8,128)(2,1)}), bf16[8,96,2048]{2,1,0:T(8,128)(2,1)S(1)}, u32[]{:S(2)}, u32[]{:S(2)}) %all-to-all-start.1) | async-done | bytes 3145760 | tf_op jit(solution)/shard_map/all_to_all | solution.py:231
  356.8 16.8 %fusion.18 = f32[768,3072]{1,0:T(8,128)S(1)} fusion(bf16[768,2048]{1,0:T(8,128)(2,1)S(1)} %bitcast.302, bf16[2048,768]{0,1:T(8,128)(2,1)} %collective-permute-done.13, bf16[2048,768]{0,1:T(8,128)(2,1)} %collective-permute-done.12, bf16[2048,768]{0,1:T(8,128)(2,1)} %collective-permute-done.11, bf16[2048,768]{0,1:T(8,128)(2,1)} %slice_dynamic-update-slice_fusion.26), kind=kOutput, calls=%fused_computation.80 | convolution fusion | flops 9714008064 | bytes 25165824 | tf_op jit(solution)/shard_map/dot_general | solution.py:47
  376.3 13.0 %multiply_convert_fusion.2 = (bf16[768,1536]{1,0:T(8,128)(2,1)}, bf16[768,1536]{1,0:T(8,128)(2,1)}, f32[768,1536]{1,0:T(8,128)}) fusion(f32[768,384]{1,0:T(8,128)} %get-tuple-element.157, f32[768,384]{1,0:T(8,128)} %get-tuple-element.158, f32[768,384]{1,0:T(8,128)} %get-tuple-element.159, f32[768,384]{1,0:T(8,128)} %get-tuple-element.152, ...), kind=kOutput, calls=%fused_computation.34 | convolution fusion | flops 4854251520 | bytes 28311552 | tf_op jit(solution)/shard_map/dot_general | solution.py:57
  400.3 16.0 %convolution_convert_fusion.9 = bf16[768,2048]{1,0:T(8,128)(2,1)} fusion(bf16[768,3072]{1,0:T(8,128)(2,1)} %slice_dynamic-update-slice_fusion.6, bf16[2048,768]{0,1:T(8,128)(2,1)} %collective-permute-done.13, bf16[2048,768]{0,1:T(8,128)(2,1)} %collective-permute-done.12, bf16[2048,768]{0,1:T(8,128)(2,1)} %collective-permute-done.11, ...), kind=kOutput, calls=%fused_computation.52 | convolution fusion | flops 9715580928 | bytes 20447232 | tf_op jit(solution)/shard_map/dot_general | solution.py:57
  416.3 13.0 %convolution_convert_fusion.1 = bf16[2048,3072]{1,0:T(8,128)(2,1)S(1)} fusion(bf16[768,2048]{1,0:T(8,128)(2,1)S(1)} %bitcast.303, bf16[768,3072]{1,0:T(8,128)(2,1)} %slice_dynamic-update-slice_fusion.6), kind=kOutput, calls=%fused_computation.2 | convolution fusion | flops 9669967872 | bytes 20447232 | tf_op jit(solution)/shard_map/dot_general | solution.py:51
  452.0 9.5 %convolution_convert_fusion.8 = bf16[768,2048]{1,0:T(8,128)(2,1)} fusion(bf16[768,1536]{1,0:T(8,128)(2,1)} %get-tuple-element.47, bf16[1536,2048]{1,0:T(8,128)(2,1)} %constant_dynamic-update-slice_fusion.30), kind=kOutput, calls=%fused_computation.51 | convolution fusion | flops 4833411072 | bytes 11796480 | tf_op jit(solution)/shard_map/dot_general | solution.py:47
  471.2 15.7 %fusion.95 = f32[768,2816]{1,0:T(8,128)} fusion(bf16[768,2048]{1,0:T(8,128)(2,1)} %copy-done.9, bf16[2048,2816]{1,0:T(8,128)(2,1)} %all-gather.9.cloned.1.call-done), kind=kOutput, calls=%fused_computation.372 | convolution fusion | flops 8858370048 | bytes 23330816 | tf_op jit(solution)/shard_map/dot_general | solution.py:47
  486.9 12.5 %multiply_convert_fusion.6 = (bf16[768,1408]{1,0:T(8,128)(2,1)S(1)}, bf16[768,1408]{1,0:T(8,128)(2,1)S(1)}, bf16[768,1408]{1,0:T(8,128)(2,1)}) fusion(f32[768,2816]{1,0:T(8,128)} %fusion.95, bf16[768,2048]{1,0:T(8,128)(2,1)} %multiply_convert_fusion.1, bf16[2048,1408]{0,1:T(8,128)(2,1)} %all-gather.11.cloned.1.call-done), kind=kOutput, calls=%fused_computation.42 | convolution fusion | flops 4445405184 | bytes 24051712 | tf_op jit(solution)/shard_map/dot_general | solution.py:47
  502.9 12.2 %convolution_convert_fusion = bf16[2048,2816]{1,0:T(8,128)(2,1)} fusion(bf16[768,2048]{1,0:T(8,128)(2,1)S(1)} %copy-done.11, bf16[768,1408]{1,0:T(8,128)(2,1)S(1)} %get-tuple-element.144, bf16[768,1408]{1,0:T(8,128)(2,1)S(1)} %get-tuple-element.143), kind=kOutput, calls=%fused_computation.1 | convolution fusion | flops 8872787968 | bytes 19005440 | tf_op jit(solution)/shard_map/dot_general | solution.py:51
  515.0 15.0 %fusion.96 = f32[768,2048]{1,0:T(8,128)} fusion(bf16[768,2816]{1,0:T(8,128)(2,1)} %pad_maximum_fusion.4, bf16[2048,2816]{1,0:T(8,128)(2,1)} %all-gather.9.cloned.1.call-done), kind=kOutput, calls=%fused_computation.373 | convolution fusion | flops 8858370048 | bytes 22151168 | tf_op jit(solution)/shard_map/dot_general | solution.py:57
  551.9 16.8 %collective-permute-done.18 = f32[6,128]{1,0:T(8,128)S(1)} collective-permute-done((f32[6,128]{1,0:T(8,128)S(1)}, f32[6,128]{1,0:T(8,128)S(1)}, u32[]{:S(2)}, u32[]{:S(2)}) %collective-permute-start.18) | collective-permute-done | bytes 3104 | tf_op jit(solution)/shard_map/ppermute | solution.py:167
  591.0 15.9 %collective-permute-done.20 = bf16[192,2048]{1,0:T(8,128)(2,1)} collective-permute-done((bf16[192,2048]{1,0:T(8,128)(2,1)S(1)}, bf16[192,2048]{1,0:T(8,128)(2,1)}, u32[]{:S(2)}, u32[]{:S(2)}) %collective-permute-start.20) | collective-permute-done | bytes 786464 | tf_op jit(solution)/shard_map/ppermute | solution.py:167
  634.5 10.4 %multiply_convert_fusion = bf16[4,768,768]{1,2,0:T(8,128)(2,1)} fusion(f32[4,768,768]{1,2,0:T(8,128)} %get-tuple-element.238, f32[4,768,768]{1,2,0:T(8,128)} %copy-done, f32[4,768]{1,0:T(4,128)} %get-tuple-element.237, f32[4,768]{1,0:T(4,128)S(1)} %log_add_fusion), kind=kLoop, calls=%fused_computation.3 | loop fusion | flops 9437184 | bytes 23617536 | tf_op jit(solution)/shard_map/convert_element_type | solution.py:63
  654.9 9.3 fusion.44
  688.5 21.6 %collective-permute-done.40 = bf16[352,2048]{1,0:T(8,128)(2,1)} collective-permute-done((bf16[352,2048]{1,0:T(8,128)(2,1)}, bf16[352,2048]{1,0:T(8,128)(2,1)}, u32[]{:S(2)}, u32[]{:S(2)}) %collective-permute-start.40) | collective-permute-done | bytes 1441824 | tf_op jit(solution)/shard_map/ppermute | solution.py:167
  787.9 23.7 %collective-permute-done.23 = bf16[192,2048]{1,0:T(8,128)(2,1)S(1)} collective-permute-done((bf16[192,2048]{1,0:T(8,128)(2,1)S(1)}, bf16[192,2048]{1,0:T(8,128)(2,1)S(1)}, u32[]{:S(2)}, u32[]{:S(2)}) %collective-permute-start.23) | collective-permute-done | bytes 786464 | tf_op jit(solution)/shard_map/ppermute | solution.py:167
  820.0 11.4 %collective-permute-done.25 = bf16[192,2048]{1,0:T(8,128)(2,1)S(1)} collective-permute-done((bf16[192,2048]{1,0:T(8,128)(2,1)S(1)}, bf16[192,2048]{1,0:T(8,128)(2,1)S(1)}, u32[]{:S(2)}, u32[]{:S(2)}) %collective-permute-start.25) | collective-permute-done | bytes 786464 | tf_op jit(solution)/shard_map/ppermute | solution.py:167
  845.2 73.6 %reduce-scatter.4.cloned.1.call-done = bf16[256,2048]{0,1:T(8,128)(2,1)} async-done(((bf16[2048,2048]{0,1:T(8,128)(2,1)}), bf16[256,2048]{0,1:T(8,128)(2,1)}) %reduce-scatter.4.cloned.1.call-update) | async-done | bytes 1048592 | tf_op jit(solution)/shard_map/reduce_scatter | solution.py:116
  (570 shorter events, 411.2 us)
Async XLA Ops:
  7.2 73.4 %all-gather.5.cloned.1.call-start = ((), (), s32[]{:S(2)}) async-start(), calls=%async_computation.7 | async-start | bytes 7077888 | tf_op jit(solution)/shard_map/all_gather | solution.py:110
  9.5 113.2 %all-gather.7.cloned.1.call-start = ((), (), s32[]{:S(2)}) async-start(), calls=%async_computation.8 | async-start | bytes 2359296 | tf_op jit(solution)/shard_map/all_gather | solution.py:110
  10.2 460.9 %all-gather.9.cloned.1.call-start = ((), (), s32[]{:S(2)}) async-start(), calls=%async_computation.9 | async-start | bytes 12976128 | tf_op jit(solution)/shard_map/all_gather | solution.py:110
  136.0 109.3 %all-to-all-start = ((bf16[8,96,2048]{2,1,0:T(8,128)(2,1)}), bf16[8,96,2048]{2,1,0:T(8,128)(2,1)}, u32[]{:S(2)}, u32[]{:S(2)}) async-start(bf16[8,96,2048]{2,1,0:T(8,128)(2,1)} %bitcast.301), calls=%async_computation | async-start | bytes 6291456 | tf_op jit(solution)/shard_map/all_to_all | solution.py:231
  189.4 70.8 %collective-permute-start.12 = (bf16[2048,768]{0,1:T(8,128)(2,1)}, bf16[2048,768]{0,1:T(8,128)(2,1)}, u32[]{:S(2)}, u32[]{:S(2)}) collective-permute-start(bf16[2048,768]{0,1:T(8,128)(2,1)} %slice_dynamic-update-slice_fusion.26), channel_id=1, source_target_pairs={{0,2},{1,3},{2,0},{3,1},{4,6},{5,7},{6,4},{7,5},{8,10},{9,11},{10,... | collective-permute-start | bytes 9437192 | tf_op jit(solution)/shard_map/ppermute | solution.py:167
  245.4 109.8 %all-to-all-start.1 = ((bf16[8,96,2048]{2,1,0:T(8,128)(2,1)}), bf16[8,96,2048]{2,1,0:T(8,128)(2,1)S(1)}, u32[]{:S(2)}, u32[]{:S(2)}) async-start(bf16[8,96,2048]{2,1,0:T(8,128)(2,1)} %bitcast.304), calls=%async_computation.1 | async-start | bytes 6291456 | tf_op jit(solution)/shard_map/all_to_all | solution.py:231
  249.8 237.1 %all-gather.11.cloned.1.call-start = ((), (), s32[]{:S(2)}) async-start(), calls=%async_computation.10 | async-start | bytes 6488064 | tf_op jit(solution)/shard_map/all_gather | solution.py:110
  249.9 59.1 %collective-permute-start.11 = (bf16[2048,768]{0,1:T(8,128)(2,1)}, bf16[2048,768]{0,1:T(8,128)(2,1)}, u32[]{:S(2)}, u32[]{:S(2)}) collective-permute-start(bf16[2048,768]{0,1:T(8,128)(2,1)} %slice_dynamic-update-slice_fusion.26), channel_id=1, source_target_pairs={{0,1},{1,0},{2,3},{3,2},{4,5},{5,4},{6,7},{7,6},{8,9},{9,8},{10,11... | collective-permute-start | bytes 9437192 | tf_op jit(solution)/shard_map/ppermute | solution.py:163
  260.2 48.7 %collective-permute-start.13 = (bf16[2048,768]{0,1:T(8,128)(2,1)}, bf16[2048,768]{0,1:T(8,128)(2,1)}, u32[]{:S(2)}, u32[]{:S(2)}) collective-permute-start(bf16[2048,768]{0,1:T(8,128)(2,1)} %collective-permute-done.12), channel_id=1, source_target_pairs={{0,1},{1,0},{2,3},{3,2},{4,5},{5,4},{6,7},{7,6},{8,9},{9,8},{10,11... | collective-permute-start | bytes 9437192 | tf_op jit(solution)/shard_map/ppermute | solution.py:163
  261.8 34.3 %collective-permute-start.6 = (bf16[352,2048]{1,0:T(8,128)(2,1)}, bf16[352,2048]{1,0:T(8,128)(2,1)}, u32[]{:S(2)}, u32[]{:S(2)}) collective-permute-start(bf16[352,2048]{1,0:T(8,128)(2,1)} %slice_dynamic-update-slice_fusion.53), channel_id=1, source_target_pairs={{0,2},{1,3},{2,0},{3,1},{4,6},{5,7},{6,4},{7,5},{8,10},{9,11},{10,... | collective-permute-start | bytes 4325384 | tf_op jit(solution)/shard_map/ppermute | solution.py:167
  263.3 37.7 %collective-permute-start.5 = (bf16[352,2048]{1,0:T(8,128)(2,1)}, bf16[352,2048]{1,0:T(8,128)(2,1)}, u32[]{:S(2)}, u32[]{:S(2)}) collective-permute-start(bf16[352,2048]{1,0:T(8,128)(2,1)} %slice_dynamic-update-slice_fusion.53), channel_id=1, source_target_pairs={{0,1},{1,0},{2,3},{3,2},{4,5},{5,4},{6,7},{7,6},{8,9},{9,8},{10,11... | collective-permute-start | bytes 4325384 | tf_op jit(solution)/shard_map/ppermute | solution.py:163
  447.4 82.6 %all-to-all-start.2 = ((bf16[8,96,2048]{2,1,0:T(8,128)(2,1)}), bf16[8,96,2048]{2,1,0:T(8,128)(2,1)}, u32[]{:S(2)}, u32[]{:S(2)}) async-start(bf16[8,96,2048]{2,1,0:T(8,128)(2,1)} %bitcast.305), calls=%async_computation.2 | async-start | bytes 6291456 | tf_op jit(solution)/shard_map/all_to_all | solution.py:231
  451.9 387.4 %reduce-scatter.8.cloned.1.call-start = ((), (), s32[]{:S(2)}) async-start(), calls=%async_computation.13 | async-start | bytes 6488064 | tf_op jit(solution)/shard_map/reduce_scatter | solution.py:116
  582.4 259.7 %reduce-scatter.6.cloned.1.call-start = ((), (), s32[]{:S(2)}) async-start(), calls=%async_computation.12 | async-start | bytes 12976128 | tf_op jit(solution)/shard_map/reduce_scatter | solution.py:116
  586.8 34.5 %collective-permute-start.39 = (bf16[2,352,2048]{2,1,0:T(8,128)(2,1)}, bf16[2,352,2048]{2,1,0:T(8,128)(2,1)}, u32[]{:S(2)}, u32[]{:S(2)}) collective-permute-start(bf16[2,352,2048]{2,1,0:T(8,128)(2,1)} %pad_maximum_fusion.5), channel_id=1, source_target_pairs={{0,1},{1,0},{2,3},{3,2},{4,5},{5,4},{6,7},{7,6},{8,9},{9,8},{10,11... | collective-permute-start | bytes 8650760 | tf_op jit(solution)/shard_map/ppermute | solution.py:163
  608.3 80.2 %collective-permute-start.37 = (bf16[2048,768]{1,0:T(8,128)(2,1)}, bf16[2048,768]{1,0:T(8,128)(2,1)}, u32[]{:S(2)}, u32[]{:S(2)}) collective-permute-start(bf16[2048,768]{1,0:T(8,128)(2,1)} %get-tuple-element.145), channel_id=1, source_target_pairs={{0,1},{1,0},{2,3},{3,2},{4,5},{5,4},{6,7},{7,6},{8,9},{9,8},{10,11... | collective-permute-start | bytes 9437192 | tf_op jit(solution)/shard_map/ppermute | solution.py:163
  608.9 79.7 %collective-permute-start.38 = (bf16[2048,768]{1,0:T(8,128)(2,1)}, bf16[2048,768]{1,0:T(8,128)(2,1)}, u32[]{:S(2)}, u32[]{:S(2)}) collective-permute-start(bf16[2048,768]{1,0:T(8,128)(2,1)} %add_convert_fusion.2), channel_id=1, source_target_pairs={{0,2},{1,3},{2,0},{3,1},{4,6},{5,7},{6,4},{7,5},{8,10},{9,11},{10,... | collective-permute-start | bytes 9437192 | tf_op jit(solution)/shard_map/ppermute | solution.py:167
  610.4 136.5 %all-to-all-start.3 = ((bf16[8,96,2048]{2,1,0:T(8,128)(2,1)}), bf16[8,96,2048]{2,1,0:T(8,128)(2,1)}, u32[]{:S(2)}, u32[]{:S(2)}) async-start(bf16[8,96,2048]{2,1,0:T(8,128)(2,1)} %bitcast.300), calls=%async_computation.3 | async-start | bytes 6291456 | tf_op jit(solution)/shard_map/all_to_all | solution.py:231
  616.1 302.6 %reduce-scatter.4.cloned.1.call-start = ((), (), s32[]{:S(2)}) async-start(), calls=%async_computation.11 | async-start | bytes 9437184 | tf_op jit(solution)/shard_map/reduce_scatter | solution.py:116
  625.1 85.1 %collective-permute-start.40 = (bf16[352,2048]{1,0:T(8,128)(2,1)}, bf16[352,2048]{1,0:T(8,128)(2,1)}, u32[]{:S(2)}, u32[]{:S(2)}) collective-permute-start(bf16[352,2048]{1,0:T(8,128)(2,1)} %fusion.14), channel_id=1, source_target_pairs={{0,2},{1,3},{2,0},{3,1},{4,6},{5,7},{6,4},{7,5},{8,10},{9,11},{10,... | collective-permute-start | bytes 4325384 | tf_op jit(solution)/shard_map/ppermute | solution.py:167
  672.7 70.2 %collective-permute-start.27 = (bf16[2,192,2048]{2,1,0:T(8,128)(2,1)}, bf16[2,192,2048]{2,1,0:T(8,128)(2,1)S(1)}, u32[]{:S(2)}, u32[]{:S(2)}) collective-permute-start(bf16[2,192,2048]{2,1,0:T(8,128)(2,1)} %dynamic-slice_bitcast_fusion), channel_id=1, source_target_pairs={{0,1},{1,0},{2,3},{3,2},{4,5},{5,4},{6,7},{7,6},{8,9},{9,8},{10,11... | collective-permute-start | bytes 4718600 | tf_op jit(solution)/shard_map/ppermute | solution.py:163
  774.8 42.2 %collective-permute-start.29 = (bf16[192,2048]{1,0:T(8,128)(2,1)S(1)}, bf16[192,2048]{1,0:T(8,128)(2,1)}, u32[]{:S(2)}, u32[]{:S(2)}) collective-permute-start(bf16[192,2048]{1,0:T(8,128)(2,1)S(1)} %slice_dynamic-update-slice_fusion.51), channel_id=1, source_target_pairs={{0,1},{1,0},{2,3},{3,2},{4,5},{5,4},{6,7},{7,6},{8,9},{9,8},{10,11... | collective-permute-start | bytes 2359304 | tf_op jit(solution)/shard_map/ppermute | solution.py:163
  774.9 39.5 %collective-permute-start.30 = (bf16[192,2048]{1,0:T(8,128)(2,1)S(1)}, bf16[192,2048]{1,0:T(8,128)(2,1)S(1)}, u32[]{:S(2)}, u32[]{:S(2)}) collective-permute-start(bf16[192,2048]{1,0:T(8,128)(2,1)S(1)} %slice_dynamic-update-slice_fusion.51), channel_id=1, source_target_pairs={{0,2},{1,3},{2,0},{3,1},{4,6},{5,7},{6,4},{7,5},{8,10},{9,11},{10,... | collective-permute-start | bytes 2359304 | tf_op jit(solution)/shard_map/ppermute | solution.py:167
  781.7 29.9 %collective-permute-start.23 = (bf16[192,2048]{1,0:T(8,128)(2,1)S(1)}, bf16[192,2048]{1,0:T(8,128)(2,1)S(1)}, u32[]{:S(2)}, u32[]{:S(2)}) collective-permute-start(bf16[192,2048]{1,0:T(8,128)(2,1)S(1)} %fusion.49), channel_id=1, source_target_pairs={{0,2},{1,3},{2,0},{3,1},{4,6},{5,7},{6,4},{7,5},{8,10},{9,11},{10,... | collective-permute-start | bytes 2359304 | tf_op jit(solution)/shard_map/ppermute | solution.py:167
  (129 other events, 1014.1 us)
Sparse Core Ops, SparseCore 0:
  10.1 70.4 all-gather.4
  82.1 40.5 all-gather.6
  124.8 241.9 all-gather.8
  368.0 76.2 all-gather.10
  582.5 103.6 reduce-scatter.7
  688.4 140.0 reduce-scatter.5
  830.7 88.0 reduce-scatter.3
where the time goes:
time: 937 us; the launch traced here: 931 us
  waiting for transfers between devices  378 us (40%)
  matrix products  222 us (24%)
  local copies, waits for them, and re-layouts  163 us (17%)
  other arithmetic  96.5 us (10%)
  starting transfers between devices  54.8 us (6%)
  between operations  17 us (2%)
    ppermute x14, waiting for transfers between devices, outer(): return lax.ppermute(values, 'tp', [(i, i ^ 2) for i in range(4)])  165 us
    all_to_all x4, waiting for transfers between devices, exchange(): return lax.all_to_all(rows, 'ep', split_axis=0, concat_axis=0, tiled=True)  92.7 us
    unnamed x291, local copies, waits for them, and re-layouts  79.5 us
    dot_general x9, matrix products, times(): return jnp.dot(left, right, preferred_element_type=jnp.float32)  74.1 us
    reduce_scatter x3, waiting for transfers between devices, ring_scatter(): lax.psum_scatter(full, 'ep', scatter_dimension=0, tiled=True, axis_index_...  73.6 us
    dot_general x8, matrix products, contract_rows(): lax.dot_general(left, right, (((0,), (0,)), ((), ())), preferred_element_...  69 us
    dot_general x6, matrix products, times_transpose(): lax.dot_general(left, right, (((1,), (1,)), ((), ())), preferred_element_...  60.4 us
    all_gather x4, waiting for transfers between devices, ring_gather(): lax.all_gather(shard, 'ep', axis=0, tiled=True, axis_index_groups=[ring_o...  40.9 us
  transfers between devices with their start and end apart: 52, of which 19 were waited for; matrix products, arithmetic and copies ran while one was open for 46% of the time, Pallas kernels for 0%

commit v1 on v0

--- a/solution.py
+++ b/solution.py
@@ -119,6 +119,20 @@
         scatter_dimension=0,
         tiled=True,
         axis_index_groups=[ring_order(lax.axis_size("ep"))],
+    )
+
+
+def mirror(values):
+    count = lax.axis_size("ep")
+    pairs = [(i, (i + count // 2) % count) for i in range(count)]
+    return lax.ppermute(values, "ep", pairs)
+
+
+def half_exchange(rows):
+    count = lax.axis_size("ep")
+    groups = [list(range(count // 2)), list(range(count // 2, count))]
+    return lax.all_to_all(
+        rows, "ep", split_axis=0, concat_axis=0, tiled=True, axis_index_groups=groups
     )
 
 
@@ -341,13 +355,44 @@
         weighted = jnp.where(hit, route_weights[:, choice][None, :], weighted)
     select, weighted = low(select), low(weighted)
 
+    half_count = ep_count // 2
+    upper = lax.axis_index("ep") >= half_count
+    half_slots = half_count * slots_here
+    here = jnp.where(upper, half_slots, 0)
+    half_ids = jnp.arange(half_slots, dtype=jnp.int32)[:, None] + here
+    mirror_target = mirror(target)
+    mirror_weights = mirror(route_weights)
+
+    def in_order(own, other):
+        return jnp.where(upper, other, own), jnp.where(upper, own, other)
+
+    picks = []
+    for targets, weights in zip(
+        in_order(target, mirror_target), in_order(route_weights, mirror_weights)
+    ):
+        pick = jnp.zeros((half_slots, row_count), jnp.float32)
+        for choice in range(top_count):
+            hit = half_ids == targets[:, choice][None, :]
+            pick = jnp.where(hit, weights[:, choice][None, :], pick)
+        picks.append(low(pick))
+
+    def packed(own, other):
+        blocks = [
+            low(times(pick, rows)).reshape(half_count, 1, slots_here, model_width)
+            for pick, rows in zip(picks, in_order(own, other))
+        ]
+        return jnp.concatenate(blocks, axis=1)
+
+    def by_block(rows):
+        rows = rows.reshape(half_count, 2, slots_here, model_width)
+        return rows.transpose(1, 0, 2, 3).reshape(experts_total, slots_here, model_width)
+
     grad_low = to_ring(cotangent, 1)
     grad_low = jnp.where(valid_rows[:, None], grad_low, jnp.zeros_like(grad_low))
     grad_out = grad_low.astype(jnp.float32)
-    grad_sent = low(times(weighted, grad_low))
-    grad_sent = grad_sent.reshape(experts_total, slots_here, model_width)
-    grad_arrived = exchange(after(grad_sent, full_qkv))
-    grad_arrived = grad_arrived.reshape(slot_rows, model_width)
+    mirror_grad = rows_gather(mirror(after(own_rows(grad_low), full_qkv)))
+    grad_sent = packed(grad_low, mirror_grad)
+    grad_arrived = by_block(half_exchange(grad_sent)).reshape(slot_rows, model_width)
 
     tokens = to_ring(tokens, 1)
     inputs = tokens.astype(jnp.float32)
@@ -397,21 +442,11 @@
     back_home = back_home.reshape(slot_rows, model_width)
     both_last, inner_last = after((both_grad, inner_act), back_rows)
     grad_in = low(contract_rows(arrived, both_last))
-    grad_in_terms, grad_in_sent = tp_reduce(
+    grad_in_terms, _ = tp_reduce(
         [grad_in[:, 2 * i * group : 2 * (i + 1) * group] for i in range(4)]
     )
-    inner_last = after(inner_last, grad_in)
-    grad_down = low(contract_rows(inner_last, grad_arrived))
-    grad_down_near = inner(
-        jnp.stack([grad_down[i * group : i * group + expert_hidden] for i in (1, 3)])
-    )
-    produced = low(times(after(inner_last, grad_down), expert_out))
-    produced_home = exchange(
-        after(produced, back_home).reshape(experts_total, slots_here, model_width)
-    )
-    produced_home = produced_home.reshape(slot_rows, model_width)
-
-    shared_rows = after(normed_two, produced, grad_in_sent)
+
+    shared_rows = after(normed_two, grad_in)
     shared_act = times(shared_rows, full_shared)
     shared_gate_act = shared_act[:, :shared_hidden]
     shared_up_act = shared_act[:, shared_hidden:]
@@ -433,6 +468,16 @@
     shared_grad = jnp.concatenate([shared_gate_grad, shared_up_grad], axis=1)
     shared_part_grad = low(contract_rows(shared_rows, shared_grad))
     grad_shared = ring_scatter(shared_part_grad)
+    inner_last = after(inner_last, shared_part_grad)
+    grad_down = low(contract_rows(inner_last, grad_arrived))
+    grad_down_near = inner(
+        jnp.stack([grad_down[i * group : i * group + expert_hidden] for i in (1, 3)])
+    )
+    produced = low(times(after(inner_last, grad_down), expert_out))
+    produced_home = exchange(
+        after(produced, back_home).reshape(experts_total, slots_here, model_width)
+    )
+    produced_home = produced_home.reshape(slot_rows, model_width)
     grad_shared_gate = grad_shared[:, :shared_hidden].astype(jnp.float32)
     grad_shared_up = grad_shared[:, shared_hidden:].astype(jnp.float32)
     shared_grad, select_then = after((shared_grad, select), shared_part_grad)

time: 937 us -> 902 us (0.963)
  waiting for transfers between devices: 378 us -> 336 us
    all_to_all x4 -> x3, waiting for transfers between devices: 92.7 us -> 13 us  [exchange(): return lax.all_to_all(rows, 'ep', split_axis=0, concat_axis=0, tiled=True)]
    reduce_scatter x3, waiting for transfers between devices: 73.6 us -> 40.5 us  [ring_scatter(): lax.psum_scatter(full, 'ep', scatter_dimension=0, tiled=True, axis_index_...]
    ppermute x14 -> x15, waiting for transfers between devices: 165 us -> 194 us  [outer(): return lax.ppermute(values, 'tp', [(i, i ^ 2) for i in range(4)])]
    all_to_all x0 -> x1, waiting for transfers between devices: none -> 18.8 us  [half_exchange(): lax.all_to_all(rows, 'ep', split_axis=0, concat_axis=0, tiled=True, axis_...]
    all_gather x4, waiting for transfers between devices: 40.9 us -> 59.7 us  [ring_gather(): lax.all_gather(shard, 'ep', axis=0, tiled=True, axis_index_groups=[ring_o...]
    unnamed x291 -> x289, local copies, waits for them, and re-layouts: 79.5 us -> 70.4 us
    all_to_all x4 -> x3, starting transfers between devices: 19.2 us -> 13.5 us  [exchange(): return lax.all_to_all(rows, 'ep', split_axis=0, concat_axis=0, tiled=True)]
    dot_general x9 -> x10, matrix products: 74.1 us -> 77.1 us  [times(): return jnp.dot(left, right, preferred_element_type=jnp.float32)]
  transfers between devices with their start and end apart: 52 -> 58, of which waited for: 19 -> 23; matrix products, arithmetic and copies ran while one was open for 46% -> 49% of each run, Pallas kernels for 0% -> 0%
where the time goes in v1:
time: 902 us; the launch traced here: 896 us
  waiting for transfers between devices  336 us (37%)
  matrix products  224 us (25%)
  local copies, waits for them, and re-layouts  160 us (18%)
  other arithmetic  101 us (11%)
  starting transfers between devices  57.8 us (6%)
  between operations  17.2 us (2%)
    ppermute x15, waiting for transfers between devices, outer(): return lax.ppermute(values, 'tp', [(i, i ^ 2) for i in range(4)])  194 us
    dot_general x10, matrix products, times(): return jnp.dot(left, right, preferred_element_type=jnp.float32)  77.1 us
    unnamed x289, local copies, waits for them, and re-layouts  70.4 us
    dot_general x6, matrix products, times_transpose(): lax.dot_general(left, right, (((1,), (1,)), ((), ())), preferred_element_...  66.7 us
    dot_general x8, matrix products, contract_rows(): lax.dot_general(left, right, (((0,), (0,)), ((), ())), preferred_element_...  62.9 us
    all_gather x4, waiting for transfers between devices, ring_gather(): lax.all_gather(shard, 'ep', axis=0, tiled=True, axis_index_groups=[ring_o...  59.7 us
    reduce_scatter x3, waiting for transfers between devices, ring_scatter(): lax.psum_scatter(full, 'ep', scatter_dimension=0, tiled=True, axis_index_...  40.5 us
    convert_element_type x9, other arithmetic, low(): return values.astype(jnp.bfloat16)  29.2 us
  transfers between devices with their start and end apart: 58, of which 23 were waited for; matrix products, arithmetic and copies ran while one was open for 49% of the time, Pallas kernels for 0%

profile of v1, /device:TPU:0, one launch (start us, length us, event | category | flops | bytes accessed | tf_op | source)
XLA Modules:
  0.0 895.8 jit_solution(2941283330659462756)
XLA Ops:
  57.7 23.2 %all-gather.5.cloned.1.call-done = bf16[2048,1536]{1,0:T(8,128)(2,1)} async-done(((bf16[256,1536]{1,0:T(8,128)(2,1)}), bf16[2048,1536]{1,0:T(8,128)(2,1)}) %all-gather.5.cloned.1.call-update) | async-done | bytes 6291472 | tf_op jit(solution)/shard_map/all_gather | solution.py:110
  104.8 36.5 %all-gather.7.cloned.1.call-done = bf16[2048,512]{0,1:T(8,128)(2,1)} async-done(((bf16[256,512]{0,1:T(8,128)(2,1)}), bf16[2048,512]{0,1:T(8,128)(2,1)}) %all-gather.7.cloned.1.call-update) | async-done | bytes 2097168 | tf_op jit(solution)/shard_map/all_gather | solution.py:110
  156.2 15.8 %collective-permute-done.9 = bf16[192,2048]{1,0:T(8,128)(2,1)S(1)} collective-permute-done((bf16[192,2048]{1,0:T(8,128)(2,1)}, bf16[192,2048]{1,0:T(8,128)(2,1)S(1)}, u32[]{:S(2)}, u32[]{:S(2)}) %collective-permute-start.9) | collective-permute-done | bytes 786464 | tf_op jit(solution)/shard_map/ppermute | solution.py:181
  192.7 14.7 %collective-permute-done.4 = bf16[192,2048]{1,0:T(8,128)(2,1)S(1)} collective-permute-done((bf16[192,2048]{1,0:T(8,128)(2,1)S(1)}, bf16[192,2048]{1,0:T(8,128)(2,1)S(1)}, u32[]{:S(2)}, u32[]{:S(2)}) %collective-permute-start.4) | collective-permute-done | bytes 786464 | tf_op jit(solution)/shard_map/ppermute | solution.py:181
  215.4 14.2 %collective-permute-done.15 = bf16[192,2048]{1,0:T(8,128)(2,1)S(1)} collective-permute-done((bf16[192,2048]{1,0:T(8,128)(2,1)S(1)}, bf16[192,2048]{1,0:T(8,128)(2,1)S(1)}, u32[]{:S(2)}, u32[]{:S(2)}) %collective-permute-start.15) | collective-permute-done | bytes 786464 | tf_op jit(solution)/shard_map/ppermute | solution.py:181
  238.2 18.8 %all-to-all-done = bf16[4,2,96,2048]{3,2,1,0:T(8,128)(2,1)} async-done(((bf16[4,2,96,2048]{3,2,1,0:T(8,128)(2,1)}), bf16[4,2,96,2048]{3,2,1,0:T(8,128)(2,1)}, u32[]{:S(2)}, u32[]{:S(2)}) %all-to-all-start) | async-done | bytes 3145760 | tf_op jit(solution)/shard_map/all_to_all | solution.py:134
  275.6 25.7 %collective-permute-done.18 = bf16[2048,768]{0,1:T(8,128)(2,1)} collective-permute-done((bf16[2048,768]{0,1:T(8,128)(2,1)}, bf16[2048,768]{0,1:T(8,128)(2,1)}, u32[]{:S(2)}, u32[]{:S(2)}) %collective-permute-start.18) | collective-permute-done | bytes 3145760 | tf_op jit(solution)/shard_map/ppermute | solution.py:181
  304.6 32.6 %collective-permute-done.12 = bf16[352,2048]{1,0:T(8,128)(2,1)} collective-permute-done((bf16[352,2048]{1,0:T(8,128)(2,1)}, bf16[352,2048]{1,0:T(8,128)(2,1)}, u32[]{:S(2)}, u32[]{:S(2)}) %collective-permute-start.12) | collective-permute-done | bytes 1441824 | tf_op jit(solution)/shard_map/ppermute | solution.py:181
  359.0 17.6 %fusion.30 = f32[768,3072]{1,0:T(8,128)S(1)} fusion(bf16[768,2048]{1,0:T(8,128)(2,1)} %bitcast.33, bf16[2048,768]{0,1:T(8,128)(2,1)} %collective-permute-done.19, bf16[2048,768]{0,1:T(8,128)(2,1)} %collective-permute-done.18, bf16[2048,768]{0,1:T(8,128)(2,1)} %collective-permute-done.17, bf16[2048,768]{0,1:T(8,128)(2,1)} %slice_dynamic-update-slice_fusion.26), kind=kOutput, calls=%fused_computation.88 | convolution fusion | flops 9714008064 | bytes 25165824 | tf_op jit(solution)/shard_map/dot_general | solution.py:47
  380.4 13.6 %multiply_convert_fusion.2 = (bf16[768,1536]{1,0:T(8,128)(2,1)}, bf16[768,1536]{1,0:T(8,128)(2,1)}, f32[768,1536]{1,0:T(8,128)}) fusion(f32[768,384]{1,0:T(8,128)} %get-tuple-element.211, f32[768,384]{1,0:T(8,128)} %get-tuple-element.212, f32[768,384]{1,0:T(8,128)} %get-tuple-element.213, f32[768,384]{1,0:T(8,128)} %get-tuple-element.206, ...), kind=kOutput, calls=%fused_computation.34 | convolution fusion | flops 4854251520 | bytes 28311552 | tf_op jit(solution)/shard_map/dot_general | solution.py:57
  406.0 15.9 %convolution_convert_fusion.8 = bf16[768,2048]{1,0:T(8,128)(2,1)} fusion(bf16[768,3072]{1,0:T(8,128)(2,1)} %slice_dynamic-update-slice_fusion.6, bf16[2048,768]{0,1:T(8,128)(2,1)} %collective-permute-done.19, bf16[2048,768]{0,1:T(8,128)(2,1)} %collective-permute-done.18, bf16[2048,768]{0,1:T(8,128)(2,1)} %collective-permute-done.17, ...), kind=kOutput, calls=%fused_computation.51 | convolution fusion | flops 9715580928 | bytes 20447232 | tf_op jit(solution)/shard_map/dot_general | solution.py:57
  421.9 15.8 %convolution_convert_fusion.1 = bf16[2048,3072]{1,0:T(8,128)(2,1)} fusion(bf16[768,2048]{1,0:T(8,128)(2,1)} %bitcast.33, bf16[768,3072]{1,0:T(8,128)(2,1)} %slice_dynamic-update-slice_fusion.6), kind=kOutput, calls=%fused_computation.2 | convolution fusion | flops 9669967872 | bytes 20447232 | tf_op jit(solution)/shard_map/dot_general | solution.py:51
  447.1 16.3 %fusion.137 = f32[768,2816]{1,0:T(8,128)} fusion(bf16[768,2048]{1,0:T(8,128)(2,1)} %copy-done.8, bf16[2048,2816]{1,0:T(8,128)(2,1)} %all-gather.11.cloned.1.call-done), kind=kOutput, calls=%fused_computation.438 | convolution fusion | flops 8858370048 | bytes 23330816 | tf_op jit(solution)/shard_map/dot_general | solution.py:47
  463.4 11.4 %multiply_convert_fusion.7 = (bf16[768,1408]{1,0:T(8,128)(2,1)S(1)}, bf16[768,1408]{1,0:T(8,128)(2,1)S(1)}, bf16[768,1408]{1,0:T(8,128)(2,1)}) fusion(f32[768,2816]{1,0:T(8,128)} %fusion.137, bf16[768,2048]{1,0:T(8,128)(2,1)S(1)} %copy-done.35, bf16[2048,1408]{0,1:T(8,128)(2,1)} %all-gather.9.cloned.1.call-done), kind=kOutput, calls=%fused_computation.43 | convolution fusion | flops 4445405184 | bytes 24051712 | tf_op jit(solution)/shard_map/dot_general | solution.py:47
  478.3 12.1 %convolution_convert_fusion = bf16[2048,2816]{1,0:T(8,128)(2,1)} fusion(bf16[768,2048]{1,0:T(8,128)(2,1)S(1)} %copy-done.9, bf16[768,1408]{1,0:T(8,128)(2,1)S(1)} %get-tuple-element.198, bf16[768,1408]{1,0:T(8,128)(2,1)S(1)} %get-tuple-element.197), kind=kOutput, calls=%fused_computation.1 | convolution fusion | flops 8872787968 | bytes 19005440 | tf_op jit(solution)/shard_map/dot_general | solution.py:51
  490.4 15.1 %fusion.138 = f32[768,2048]{1,0:T(8,128)} fusion(bf16[768,2816]{1,0:T(8,128)(2,1)} %pad_maximum_fusion.4, bf16[2048,2816]{1,0:T(8,128)(2,1)} %all-gather.11.cloned.1.call-done), kind=kOutput, calls=%fused_computation.439 | convolution fusion | flops 8858370048 | bytes 22151168 | tf_op jit(solution)/shard_map/dot_general | solution.py:57
  523.2 9.9 %multiply_reduce_fusion.1 = (f32[768]{0:T(1024)S(1)}, f32[768,2048]{1,0:T(8,128)}) fusion(bf16[768,2048]{1,0:T(8,128)(2,1)S(1)} %copy-done.7, bf16[768,1408]{1,0:T(8,128)(2,1)S(1)} %copy-done.91, bf16[2048,1408]{0,1:T(8,128)(2,1)} %all-gather.9.cloned.1.call-done), kind=kOutput, calls=%fused_computation.22 | convolution fusion | flops 4433902592 | bytes 17370112 | tf_op jit(solution)/shard_map/dot_general | solution.py:57
  571.6 11.6 %convolution_convert_fusion.7 = bf16[768,2048]{1,0:T(8,128)(2,1)} fusion(bf16[768,1536]{1,0:T(8,128)(2,1)S(1)} %copy-done.92, bf16[1536,2048]{1,0:T(8,128)(2,1)} %constant_dynamic-update-slice_fusion.30), kind=kOutput, calls=%fused_computation.50 | convolution fusion | flops 4833411072 | bytes 11796480 | tf_op jit(solution)/shard_map/dot_general | solution.py:47
  587.1 15.5 %collective-permute-done.25 = bf16[192,2048]{1,0:T(8,128)(2,1)} collective-permute-done((bf16[192,2048]{1,0:T(8,128)(2,1)S(1)}, bf16[192,2048]{1,0:T(8,128)(2,1)}, u32[]{:S(2)}, u32[]{:S(2)}) %collective-permute-start.25) | collective-permute-done | bytes 786464 | tf_op jit(solution)/shard_map/ppermute | solution.py:181
  629.7 10.3 %multiply_convert_fusion = bf16[4,768,768]{1,2,0:T(8,128)(2,1)} fusion(f32[4,768,768]{1,2,0:T(8,128)} %get-tuple-element.296, f32[4,768,768]{1,2,0:T(8,128)} %copy-done, f32[4,768]{1,0:T(4,128)S(1)} %get-tuple-element.295, f32[4,768]{1,0:T(4,128)S(1)} %log_add_fusion), kind=kLoop, calls=%fused_computation.3 | loop fusion | flops 9437184 | bytes 23617536 | tf_op jit(solution)/shard_map/convert_element_type | solution.py:63
  688.1 20.9 %collective-permute-done.46 = bf16[352,2048]{1,0:T(8,128)(2,1)} collective-permute-done((bf16[352,2048]{1,0:T(8,128)(2,1)}, bf16[352,2048]{1,0:T(8,128)(2,1)}, u32[]{:S(2)}, u32[]{:S(2)}) %collective-permute-start.46) | collective-permute-done | bytes 1441824 | tf_op jit(solution)/shard_map/ppermute | solution.py:181
  785.8 24.8 %collective-permute-done.28 = bf16[192,2048]{1,0:T(8,128)(2,1)S(1)} collective-permute-done((bf16[192,2048]{1,0:T(8,128)(2,1)S(1)}, bf16[192,2048]{1,0:T(8,128)(2,1)S(1)}, u32[]{:S(2)}, u32[]{:S(2)}) %collective-permute-start.28) | collective-permute-done | bytes 786464 | tf_op jit(solution)/shard_map/ppermute | solution.py:181
  819.1 11.2 %collective-permute-done.30 = bf16[192,2048]{1,0:T(8,128)(2,1)S(1)} collective-permute-done((bf16[192,2048]{1,0:T(8,128)(2,1)S(1)}, bf16[192,2048]{1,0:T(8,128)(2,1)S(1)}, u32[]{:S(2)}, u32[]{:S(2)}) %collective-permute-start.30) | collective-permute-done | bytes 786464 | tf_op jit(solution)/shard_map/ppermute | solution.py:181
  842.9 40.5 %reduce-scatter.4.cloned.1.call-done = bf16[256,2048]{0,1:T(8,128)(2,1)} async-done(((bf16[2048,2048]{0,1:T(8,128)(2,1)}), bf16[256,2048]{0,1:T(8,128)(2,1)}) %reduce-scatter.4.cloned.1.call-update) | async-done | bytes 1048592 | tf_op jit(solution)/shard_map/reduce_scatter | solution.py:116
  (592 shorter events, 434.6 us)
Async XLA Ops:
  7.2 73.7 %all-gather.5.cloned.1.call-start = ((), (), s32[]{:S(2)}) async-start(), calls=%async_computation.7 | async-start | bytes 7077888 | tf_op jit(solution)/shard_map/all_gather | solution.py:110
  9.5 131.8 %all-gather.7.cloned.1.call-start = ((), (), s32[]{:S(2)}) async-start(), calls=%async_computation.8 | async-start | bytes 2359296 | tf_op jit(solution)/shard_map/all_gather | solution.py:110
  10.2 436.9 %all-gather.11.cloned.1.call-start = ((), (), s32[]{:S(2)}) async-start(), calls=%async_computation.10 | async-start | bytes 12976128 | tf_op jit(solution)/shard_map/all_gather | solution.py:110
  17.6 136.0 %collective-permute-start.6 = (f32[768,4]{0,1:T(4,128)}, f32[768,4]{0,1:T(4,128)}, u32[]{:S(2)}, u32[]{:S(2)}) collective-permute-start(f32[768,4]{0,1:T(4,128)} %param.25), channel_id=1, source_target_pairs={{0,16},{4,20},{8,24},{12,28},{16,0},{20,4},{24,8},{28,12},{1,17},{... | collective-permute-start | bytes 36872 | tf_op jit(solution)/shard_map/ppermute | solution.py:128
  80.9 71.2 %collective-permute-start.7 = (bf16[192,2048]{1,0:T(8,128)(2,1)}, bf16[192,2048]{1,0:T(8,128)(2,1)}, u32[]{:S(2)}, u32[]{:S(2)}) collective-permute-start(bf16[192,2048]{1,0:T(8,128)(2,1)} %constant_dynamic-slice_fusion.4), channel_id=1, source_target_pairs={{0,16},{4,20},{8,24},{12,28},{16,0},{20,4},{24,8},{28,12},{1,17},{... | collective-permute-start | bytes 2359304 | tf_op jit(solution)/shard_map/ppermute | solution.py:128
  181.2 75.9 %all-to-all-start = ((bf16[4,2,96,2048]{3,2,1,0:T(8,128)(2,1)}), bf16[4,2,96,2048]{3,2,1,0:T(8,128)(2,1)}, u32[]{:S(2)}, u32[]{:S(2)}) async-start(bf16[4,2,96,2048]{3,2,1,0:T(8,128)(2,1)} %pad_maximum_fusion.5), calls=%async_computation | async-start | bytes 6291456 | tf_op jit(solution)/shard_map/all_to_all | solution.py:134
  230.5 70.8 %collective-permute-start.18 = (bf16[2048,768]{0,1:T(8,128)(2,1)}, bf16[2048,768]{0,1:T(8,128)(2,1)}, u32[]{:S(2)}, u32[]{:S(2)}) collective-permute-start(bf16[2048,768]{0,1:T(8,128)(2,1)} %slice_dynamic-update-slice_fusion.26), channel_id=1, source_target_pairs={{0,2},{1,3},{2,0},{3,1},{4,6},{5,7},{6,4},{7,5},{8,10},{9,11},{10,... | collective-permute-start | bytes 9437192 | tf_op jit(solution)/shard_map/ppermute | solution.py:181
  261.1 97.9 %all-to-all-start.1 = ((bf16[8,96,2048]{2,1,0:T(8,128)(2,1)}), bf16[8,96,2048]{2,1,0:T(8,128)(2,1)}, u32[]{:S(2)}, u32[]{:S(2)}) async-start(bf16[8,96,2048]{2,1,0:T(8,128)(2,1)} %bitcast.310), calls=%async_computation.1 | async-start | bytes 6291456 | tf_op jit(solution)/shard_map/all_to_all | solution.py:245
  265.6 197.9 %all-gather.9.cloned.1.call-start = ((), (), s32[]{:S(2)}) async-start(), calls=%async_computation.9 | async-start | bytes 6488064 | tf_op jit(solution)/shard_map/all_gather | solution.py:110
  265.8 86.3 %collective-permute-start.17 = (bf16[2048,768]{0,1:T(8,128)(2,1)}, bf16[2048,768]{0,1:T(8,128)(2,1)}, u32[]{:S(2)}, u32[]{:S(2)}) collective-permute-start(bf16[2048,768]{0,1:T(8,128)(2,1)} %slice_dynamic-update-slice_fusion.26), channel_id=1, source_target_pairs={{0,1},{1,0},{2,3},{3,2},{4,5},{5,4},{6,7},{7,6},{8,9},{9,8},{10,11... | collective-permute-start | bytes 9437192 | tf_op jit(solution)/shard_map/ppermute | solution.py:177
  301.3 50.8 %collective-permute-start.19 = (bf16[2048,768]{0,1:T(8,128)(2,1)}, bf16[2048,768]{0,1:T(8,128)(2,1)}, u32[]{:S(2)}, u32[]{:S(2)}) collective-permute-start(bf16[2048,768]{0,1:T(8,128)(2,1)} %collective-permute-done.18), channel_id=1, source_target_pairs={{0,1},{1,0},{2,3},{3,2},{4,5},{5,4},{6,7},{7,6},{8,9},{9,8},{10,11... | collective-permute-start | bytes 9437192 | tf_op jit(solution)/shard_map/ppermute | solution.py:177
  304.4 39.8 %collective-permute-start.11 = (bf16[352,2048]{1,0:T(8,128)(2,1)}, bf16[352,2048]{1,0:T(8,128)(2,1)}, u32[]{:S(2)}, u32[]{:S(2)}) collective-permute-start(bf16[352,2048]{1,0:T(8,128)(2,1)} %slice_dynamic-update-slice_fusion.53), channel_id=1, source_target_pairs={{0,1},{1,0},{2,3},{3,2},{4,5},{5,4},{6,7},{7,6},{8,9},{9,8},{10,11... | collective-permute-start | bytes 4325384 | tf_op jit(solution)/shard_map/ppermute | solution.py:177
  437.7 73.9 %all-to-all-start.2 = ((bf16[8,96,2048]{2,1,0:T(8,128)(2,1)}), bf16[8,96,2048]{2,1,0:T(8,128)(2,1)}, u32[]{:S(2)}, u32[]{:S(2)}) async-start(bf16[8,96,2048]{2,1,0:T(8,128)(2,1)} %bitcast.311), calls=%async_computation.2 | async-start | bytes 6291456 | tf_op jit(solution)/shard_map/all_to_all | solution.py:245
  442.2 394.9 %reduce-scatter.8.cloned.1.call-start = ((), (), s32[]{:S(2)}) async-start(), calls=%async_computation.13 | async-start | bytes 6488064 | tf_op jit(solution)/shard_map/reduce_scatter | solution.py:116
  555.0 284.8 %reduce-scatter.6.cloned.1.call-start = ((), (), s32[]{:S(2)}) async-start(), calls=%async_computation.12 | async-start | bytes 12976128 | tf_op jit(solution)/shard_map/reduce_scatter | solution.py:116
  565.0 37.6 %collective-permute-start.43 = (bf16[2048,768]{1,0:T(8,128)(2,1)S(1)}, bf16[2048,768]{1,0:T(8,128)(2,1)S(1)}, u32[]{:S(2)}, u32[]{:S(2)}) collective-permute-start(bf16[2048,768]{1,0:T(8,128)(2,1)S(1)} %get-tuple-element.199), channel_id=1, source_target_pairs={{0,1},{1,0},{2,3},{3,2},{4,5},{5,4},{6,7},{7,6},{8,9},{9,8},{10,11... | collective-permute-start | bytes 9437192 | tf_op jit(solution)/shard_map/ppermute | solution.py:177
  571.6 116.5 %collective-permute-start.42 = (bf16[2048,768]{1,0:T(8,128)(2,1)}, bf16[2048,768]{1,0:T(8,128)(2,1)}, u32[]{:S(2)}, u32[]{:S(2)}) collective-permute-start(bf16[2048,768]{1,0:T(8,128)(2,1)} %get-tuple-element.200), channel_id=1, source_target_pairs={{0,1},{1,0},{2,3},{3,2},{4,5},{5,4},{6,7},{7,6},{8,9},{9,8},{10,11... | collective-permute-start | bytes 9437192 | tf_op jit(solution)/shard_map/ppermute | solution.py:177
  586.7 84.4 %collective-permute-start.45 = (bf16[2,352,2048]{2,1,0:T(8,128)(2,1)}, bf16[2,352,2048]{2,1,0:T(8,128)(2,1)}, u32[]{:S(2)}, u32[]{:S(2)}) collective-permute-start(bf16[2,352,2048]{2,1,0:T(8,128)(2,1)} %pad_maximum_fusion.6), channel_id=1, source_target_pairs={{0,1},{1,0},{2,3},{3,2},{4,5},{5,4},{6,7},{7,6},{8,9},{9,8},{10,11... | collective-permute-start | bytes 8650760 | tf_op jit(solution)/shard_map/ppermute | solution.py:177
  607.1 81.0 %collective-permute-start.44 = (bf16[2048,768]{1,0:T(8,128)(2,1)}, bf16[2048,768]{1,0:T(8,128)(2,1)}, u32[]{:S(2)}, u32[]{:S(2)}) collective-permute-start(bf16[2048,768]{1,0:T(8,128)(2,1)} %add_convert_fusion), channel_id=1, source_target_pairs={{0,2},{1,3},{2,0},{3,1},{4,6},{5,7},{6,4},{7,5},{8,10},{9,11},{10,... | collective-permute-start | bytes 9437192 | tf_op jit(solution)/shard_map/ppermute | solution.py:181
  608.8 138.5 %all-to-all-start.3 = ((bf16[8,96,2048]{2,1,0:T(8,128)(2,1)}), bf16[8,96,2048]{2,1,0:T(8,128)(2,1)}, u32[]{:S(2)}, u32[]{:S(2)}) async-start(bf16[8,96,2048]{2,1,0:T(8,128)(2,1)} %bitcast.309), calls=%async_computation.3 | async-start | bytes 6291456 | tf_op jit(solution)/shard_map/all_to_all | solution.py:245
  613.4 270.0 %reduce-scatter.4.cloned.1.call-start = ((), (), s32[]{:S(2)}) async-start(), calls=%async_computation.11 | async-start | bytes 9437184 | tf_op jit(solution)/shard_map/reduce_scatter | solution.py:116
  670.3 71.6 %collective-permute-start.32 = (bf16[2,192,2048]{2,1,0:T(8,128)(2,1)}, bf16[2,192,2048]{2,1,0:T(8,128)(2,1)}, u32[]{:S(2)}, u32[]{:S(2)}) collective-permute-start(bf16[2,192,2048]{2,1,0:T(8,128)(2,1)} %dynamic-slice_bitcast_fusion), channel_id=1, source_target_pairs={{0,1},{1,0},{2,3},{3,2},{4,5},{5,4},{6,7},{7,6},{8,9},{9,8},{10,11... | collective-permute-start | bytes 4718600 | tf_op jit(solution)/shard_map/ppermute | solution.py:177
  773.7 41.2 %collective-permute-start.34 = (bf16[192,2048]{1,0:T(8,128)(2,1)S(1)}, bf16[192,2048]{1,0:T(8,128)(2,1)}, u32[]{:S(2)}, u32[]{:S(2)}) collective-permute-start(bf16[192,2048]{1,0:T(8,128)(2,1)S(1)} %slice_dynamic-update-slice_fusion.51), channel_id=1, source_target_pairs={{0,1},{1,0},{2,3},{3,2},{4,5},{5,4},{6,7},{7,6},{8,9},{9,8},{10,11... | collective-permute-start | bytes 2359304 | tf_op jit(solution)/shard_map/ppermute | solution.py:177
  773.8 38.6 %collective-permute-start.35 = (bf16[192,2048]{1,0:T(8,128)(2,1)S(1)}, bf16[192,2048]{1,0:T(8,128)(2,1)}, u32[]{:S(2)}, u32[]{:S(2)}) collective-permute-start(bf16[192,2048]{1,0:T(8,128)(2,1)S(1)} %slice_dynamic-update-slice_fusion.51), channel_id=1, source_target_pairs={{0,2},{1,3},{2,0},{3,1},{4,6},{5,7},{6,4},{7,5},{8,10},{9,11},{10,... | collective-permute-start | bytes 2359304 | tf_op jit(solution)/shard_map/ppermute | solution.py:181
  (134 other events, 2042.0 us)
Sparse Core Ops, SparseCore 0:
  10.1 70.7 all-gather.4
  82.3 58.8 all-gather.6
  143.3 194.9 all-gather.10
  339.6 74.0 all-gather.8
  555.1 62.2 reduce-scatter.7
  619.5 166.1 reduce-scatter.5
  788.0 95.4 reduce-scatter.3

commit v2 on v1

--- a/solution.py
+++ b/solution.py
@@ -440,13 +440,7 @@
     back_rows = low(times_transpose(both_grad, expert_in))
     back_home = exchange(back_rows.reshape(experts_total, slots_here, model_width))
     back_home = back_home.reshape(slot_rows, model_width)
-    both_last, inner_last = after((both_grad, inner_act), back_rows)
-    grad_in = low(contract_rows(arrived, both_last))
-    grad_in_terms, _ = tp_reduce(
-        [grad_in[:, 2 * i * group : 2 * (i + 1) * group] for i in range(4)]
-    )
-
-    shared_rows = after(normed_two, grad_in)
+    shared_rows = after(normed_two, back_rows)
     shared_act = times(shared_rows, full_shared)
     shared_gate_act = shared_act[:, :shared_hidden]
     shared_up_act = shared_act[:, shared_hidden:]
@@ -468,7 +462,13 @@
     shared_grad = jnp.concatenate([shared_gate_grad, shared_up_grad], axis=1)
     shared_part_grad = low(contract_rows(shared_rows, shared_grad))
     grad_shared = ring_scatter(shared_part_grad)
-    inner_last = after(inner_last, shared_part_grad)
+    both_last, inner_last = after((both_grad, inner_act), shared_part_grad)
+    grad_in = low(contract_rows(arrived, both_last))
+    grad_in_terms, _ = tp_reduce(
+        [grad_in[:, 2 * i * group : 2 * (i + 1) * group] for i in range(4)]
+    )
+
+    inner_last = after(inner_last, grad_in)
     grad_down = low(contract_rows(inner_last, grad_arrived))
     grad_down_near = inner(
         jnp.stack([grad_down[i * group : i * group + expert_hidden] for i in (1, 3)])

time: 902 us -> 894 us (level)
    ppermute x15, waiting for transfers between devices: 194 us -> 203 us  [outer(): return lax.ppermute(values, 'tp', [(i, i ^ 2) for i in range(4)])]
    unnamed x289 -> x291, local copies, waits for them, and re-layouts: 70.4 us -> 69.9 us
  transfers between devices with their start and end apart: 58 -> 58, of which waited for: 23 -> 23; matrix products, arithmetic and copies ran while one was open for 49% -> 48% of each run, Pallas kernels for 0% -> 0%
where the time goes in v2:
time: 894 us; the launch traced here: 888 us
  waiting for transfers between devices  342 us (38%)
  matrix products  216 us (24%)
  local copies, waits for them, and re-layouts  156 us (17%)
  other arithmetic  100 us (11%)
  starting transfers between devices  57.3 us (6%)
  between operations  17.3 us (2%)
    ppermute x15, waiting for transfers between devices, outer(): return lax.ppermute(values, 'tp', [(i, i ^ 2) for i in range(4)])  203 us
    dot_general x10, matrix products, times(): return jnp.dot(left, right, preferred_element_type=jnp.float32)  78.1 us
    unnamed x291, local copies, waits for them, and re-layouts  69.9 us
    dot_general x6, matrix products, times_transpose(): lax.dot_general(left, right, (((1,), (1,)), ((), ())), preferred_element_...  60.9 us
    all_gather x4, waiting for transfers between devices, ring_gather(): lax.all_gather(shard, 'ep', axis=0, tiled=True, axis_index_groups=[ring_o...  59.9 us
    dot_general x8, matrix products, contract_rows(): lax.dot_general(left, right, (((0,), (0,)), ((), ())), preferred_element_...  59.9 us
    reduce_scatter x3, waiting for transfers between devices, ring_scatter(): lax.psum_scatter(full, 'ep', scatter_dimension=0, tiled=True, axis_index_...  37.1 us
    convert_element_type x9, other arithmetic, low(): return values.astype(jnp.bfloat16)  29 us
  transfers between devices with their start and end apart: 58, of which 23 were waited for; matrix products, arithmetic and copies ran while one was open for 48% of the time, Pallas kernels for 0%

profile of v2, /device:TPU:0, one launch (start us, length us, event | category | flops | bytes accessed | tf_op | source)
XLA Modules:
  0.0 888.4 jit_solution(11971249732984596462)
XLA Ops:
  57.5 23.4 %all-gather.5.cloned.1.call-done = bf16[2048,1536]{1,0:T(8,128)(2,1)} async-done(((bf16[256,1536]{1,0:T(8,128)(2,1)}), bf16[2048,1536]{1,0:T(8,128)(2,1)}) %all-gather.5.cloned.1.call-update) | async-done | bytes 6291472 | tf_op jit(solution)/shard_map/all_gather | solution.py:110
  104.8 36.5 %all-gather.7.cloned.1.call-done = bf16[2048,512]{0,1:T(8,128)(2,1)} async-done(((bf16[256,512]{0,1:T(8,128)(2,1)}), bf16[2048,512]{0,1:T(8,128)(2,1)}) %all-gather.7.cloned.1.call-update) | async-done | bytes 2097168 | tf_op jit(solution)/shard_map/all_gather | solution.py:110
  156.2 15.8 %collective-permute-done.9 = bf16[192,2048]{1,0:T(8,128)(2,1)S(1)} collective-permute-done((bf16[192,2048]{1,0:T(8,128)(2,1)}, bf16[192,2048]{1,0:T(8,128)(2,1)S(1)}, u32[]{:S(2)}, u32[]{:S(2)}) %collective-permute-start.9) | collective-permute-done | bytes 786464 | tf_op jit(solution)/shard_map/ppermute | solution.py:181
  192.6 14.7 %collective-permute-done.4 = bf16[192,2048]{1,0:T(8,128)(2,1)S(1)} collective-permute-done((bf16[192,2048]{1,0:T(8,128)(2,1)S(1)}, bf16[192,2048]{1,0:T(8,128)(2,1)S(1)}, u32[]{:S(2)}, u32[]{:S(2)}) %collective-permute-start.4) | collective-permute-done | bytes 786464 | tf_op jit(solution)/shard_map/ppermute | solution.py:181
  215.1 14.3 %collective-permute-done.15 = bf16[192,2048]{1,0:T(8,128)(2,1)S(1)} collective-permute-done((bf16[192,2048]{1,0:T(8,128)(2,1)S(1)}, bf16[192,2048]{1,0:T(8,128)(2,1)S(1)}, u32[]{:S(2)}, u32[]{:S(2)}) %collective-permute-start.15) | collective-permute-done | bytes 786464 | tf_op jit(solution)/shard_map/ppermute | solution.py:181
  238.0 18.9 %all-to-all-done = bf16[4,2,96,2048]{3,2,1,0:T(8,128)(2,1)} async-done(((bf16[4,2,96,2048]{3,2,1,0:T(8,128)(2,1)}), bf16[4,2,96,2048]{3,2,1,0:T(8,128)(2,1)}, u32[]{:S(2)}, u32[]{:S(2)}) %all-to-all-start) | async-done | bytes 3145760 | tf_op jit(solution)/shard_map/all_to_all | solution.py:134
  275.5 25.6 %collective-permute-done.18 = bf16[2048,768]{0,1:T(8,128)(2,1)} collective-permute-done((bf16[2048,768]{0,1:T(8,128)(2,1)}, bf16[2048,768]{0,1:T(8,128)(2,1)}, u32[]{:S(2)}, u32[]{:S(2)}) %collective-permute-start.18) | collective-permute-done | bytes 3145760 | tf_op jit(solution)/shard_map/ppermute | solution.py:181
  304.3 32.6 %collective-permute-done.12 = bf16[352,2048]{1,0:T(8,128)(2,1)} collective-permute-done((bf16[352,2048]{1,0:T(8,128)(2,1)}, bf16[352,2048]{1,0:T(8,128)(2,1)}, u32[]{:S(2)}, u32[]{:S(2)}) %collective-permute-start.12) | collective-permute-done | bytes 1441824 | tf_op jit(solution)/shard_map/ppermute | solution.py:181
  358.9 17.6 %fusion.30 = f32[768,3072]{1,0:T(8,128)S(1)} fusion(bf16[768,2048]{1,0:T(8,128)(2,1)} %bitcast.33, bf16[2048,768]{0,1:T(8,128)(2,1)} %collective-permute-done.19, bf16[2048,768]{0,1:T(8,128)(2,1)} %collective-permute-done.18, bf16[2048,768]{0,1:T(8,128)(2,1)} %collective-permute-done.17, bf16[2048,768]{0,1:T(8,128)(2,1)} %slice_dynamic-update-slice_fusion.26), kind=kOutput, calls=%fused_computation.88 | convolution fusion | flops 9714008064 | bytes 25165824 | tf_op jit(solution)/shard_map/dot_general | solution.py:47
  380.3 13.6 %multiply_convert_fusion.2 = (bf16[768,1536]{1,0:T(8,128)(2,1)}, bf16[768,1536]{1,0:T(8,128)(2,1)}, f32[768,1536]{1,0:T(8,128)}) fusion(f32[768,384]{1,0:T(8,128)} %get-tuple-element.211, f32[768,384]{1,0:T(8,128)} %get-tuple-element.212, f32[768,384]{1,0:T(8,128)} %get-tuple-element.213, f32[768,384]{1,0:T(8,128)} %get-tuple-element.206, ...), kind=kOutput, calls=%fused_computation.34 | convolution fusion | flops 4854251520 | bytes 28311552 | tf_op jit(solution)/shard_map/dot_general | solution.py:57
  407.1 16.0 %convolution_convert_fusion.8 = bf16[768,2048]{1,0:T(8,128)(2,1)} fusion(bf16[768,3072]{1,0:T(8,128)(2,1)} %slice_dynamic-update-slice_fusion.6, bf16[2048,768]{0,1:T(8,128)(2,1)} %collective-permute-done.19, bf16[2048,768]{0,1:T(8,128)(2,1)} %collective-permute-done.18, bf16[2048,768]{0,1:T(8,128)(2,1)} %collective-permute-done.17, ...), kind=kOutput, calls=%fused_computation.51 | convolution fusion | flops 9715580928 | bytes 20447232 | tf_op jit(solution)/shard_map/dot_general | solution.py:57
  433.0 15.8 %fusion.137 = f32[768,2816]{1,0:T(8,128)} fusion(bf16[768,2048]{1,0:T(8,128)(2,1)} %copy-done.5, bf16[2048,2816]{1,0:T(8,128)(2,1)} %all-gather.11.cloned.1.call-done), kind=kOutput, calls=%fused_computation.438 | convolution fusion | flops 8858370048 | bytes 23330816 | tf_op jit(solution)/shard_map/dot_general | solution.py:47
  448.8 12.5 %multiply_convert_fusion.7 = (bf16[768,1408]{1,0:T(8,128)(2,1)S(1)}, bf16[768,1408]{1,0:T(8,128)(2,1)S(1)}, bf16[768,1408]{1,0:T(8,128)(2,1)}) fusion(f32[768,2816]{1,0:T(8,128)} %fusion.137, bf16[768,2048]{1,0:T(8,128)(2,1)} %multiply_convert_fusion.1, bf16[2048,1408]{0,1:T(8,128)(2,1)} %all-gather.9.cloned.1.call-done), kind=kOutput, calls=%fused_computation.43 | convolution fusion | flops 4445405184 | bytes 24051712 | tf_op jit(solution)/shard_map/dot_general | solution.py:47
  464.7 12.0 %convolution_convert_fusion.1 = bf16[2048,2816]{1,0:T(8,128)(2,1)} fusion(bf16[768,2048]{1,0:T(8,128)(2,1)S(1)} %copy-done.6, bf16[768,1408]{1,0:T(8,128)(2,1)S(1)} %get-tuple-element.198, bf16[768,1408]{1,0:T(8,128)(2,1)S(1)} %get-tuple-element.197), kind=kOutput, calls=%fused_computation.2 | convolution fusion | flops 8872787968 | bytes 19005440 | tf_op jit(solution)/shard_map/dot_general | solution.py:51
  476.7 15.1 %fusion.138 = f32[768,2048]{1,0:T(8,128)} fusion(bf16[768,2816]{1,0:T(8,128)(2,1)} %pad_maximum_fusion.4, bf16[2048,2816]{1,0:T(8,128)(2,1)} %all-gather.11.cloned.1.call-done), kind=kOutput, calls=%fused_computation.439 | convolution fusion | flops 8858370048 | bytes 22151168 | tf_op jit(solution)/shard_map/dot_general | solution.py:57
  543.5 13.1 %convolution_convert_fusion = bf16[2048,3072]{1,0:T(8,128)(2,1)S(1)} fusion(bf16[768,2048]{1,0:T(8,128)(2,1)} %bitcast.33, bf16[768,3072]{1,0:T(8,128)(2,1)} %slice_dynamic-update-slice_fusion.6), kind=kOutput, calls=%fused_computation.1 | convolution fusion | flops 9669967872 | bytes 20447232 | tf_op jit(solution)/shard_map/dot_general | solution.py:51
  567.0 11.6 %convolution_convert_fusion.7 = bf16[768,2048]{1,0:T(8,128)(2,1)} fusion(bf16[768,1536]{1,0:T(8,128)(2,1)S(1)} %copy-done.89, bf16[1536,2048]{1,0:T(8,128)(2,1)} %constant_dynamic-update-slice_fusion.30), kind=kOutput, calls=%fused_computation.50 | convolution fusion | flops 4833411072 | bytes 11796480 | tf_op jit(solution)/shard_map/dot_general | solution.py:47
  582.8 14.7 %collective-permute-done.25 = bf16[192,2048]{1,0:T(8,128)(2,1)S(1)} collective-permute-done((bf16[192,2048]{1,0:T(8,128)(2,1)S(1)}, bf16[192,2048]{1,0:T(8,128)(2,1)S(1)}, u32[]{:S(2)}, u32[]{:S(2)}) %collective-permute-start.25) | collective-permute-done | bytes 786464 | tf_op jit(solution)/shard_map/ppermute | solution.py:181
  622.2 10.5 %multiply_convert_fusion = bf16[4,768,768]{1,2,0:T(8,128)(2,1)} fusion(f32[4,768,768]{1,2,0:T(8,128)} %get-tuple-element.296, f32[4,768,768]{1,2,0:T(8,128)} %copy-done, f32[4,768]{1,0:T(4,128)S(1)} %get-tuple-element.295, f32[4,768]{1,0:T(4,128)S(1)} %log_add_fusion), kind=kLoop, calls=%fused_computation.3 | loop fusion | flops 9437184 | bytes 23617536 | tf_op jit(solution)/shard_map/convert_element_type | solution.py:63
  675.5 26.6 %collective-permute-done.46 = bf16[352,2048]{1,0:T(8,128)(2,1)} collective-permute-done((bf16[352,2048]{1,0:T(8,128)(2,1)}, bf16[352,2048]{1,0:T(8,128)(2,1)}, u32[]{:S(2)}, u32[]{:S(2)}) %collective-permute-start.46) | collective-permute-done | bytes 1441824 | tf_op jit(solution)/shard_map/ppermute | solution.py:181
  738.8 9.9 %collective-permute-done.33 = bf16[192,2048]{1,0:T(8,128)(2,1)} collective-permute-done((bf16[192,2048]{1,0:T(8,128)(2,1)}, bf16[192,2048]{1,0:T(8,128)(2,1)}, u32[]{:S(2)}, u32[]{:S(2)}) %collective-permute-start.33) | collective-permute-done | bytes 786464 | tf_op jit(solution)/shard_map/ppermute | solution.py:181
  773.2 25.4 %collective-permute-done.28 = bf16[192,2048]{1,0:T(8,128)(2,1)S(1)} collective-permute-done((bf16[192,2048]{1,0:T(8,128)(2,1)S(1)}, bf16[192,2048]{1,0:T(8,128)(2,1)S(1)}, u32[]{:S(2)}, u32[]{:S(2)}) %collective-permute-start.28) | collective-permute-done | bytes 786464 | tf_op jit(solution)/shard_map/ppermute | solution.py:181
  810.8 12.4 %collective-permute-done.30 = bf16[192,2048]{1,0:T(8,128)(2,1)} collective-permute-done((bf16[192,2048]{1,0:T(8,128)(2,1)}, bf16[192,2048]{1,0:T(8,128)(2,1)}, u32[]{:S(2)}, u32[]{:S(2)}) %collective-permute-start.30) | collective-permute-done | bytes 786464 | tf_op jit(solution)/shard_map/ppermute | solution.py:181
  838.8 37.1 %reduce-scatter.4.cloned.1.call-done = bf16[256,2048]{0,1:T(8,128)(2,1)} async-done(((bf16[2048,2048]{0,1:T(8,128)(2,1)}), bf16[256,2048]{0,1:T(8,128)(2,1)}) %reduce-scatter.4.cloned.1.call-update) | async-done | bytes 1048592 | tf_op jit(solution)/shard_map/reduce_scatter | solution.py:116
  (596 shorter events, 425.4 us)
Async XLA Ops:
  7.2 73.7 %all-gather.5.cloned.1.call-start = ((), (), s32[]{:S(2)}) async-start(), calls=%async_computation.7 | async-start | bytes 7077888 | tf_op jit(solution)/shard_map/all_gather | solution.py:110
  9.5 131.8 %all-gather.7.cloned.1.call-start = ((), (), s32[]{:S(2)}) async-start(), calls=%async_computation.8 | async-start | bytes 2359296 | tf_op jit(solution)/shard_map/all_gather | solution.py:110
  10.2 422.8 %all-gather.11.cloned.1.call-start = ((), (), s32[]{:S(2)}) async-start(), calls=%async_computation.10 | async-start | bytes 12976128 | tf_op jit(solution)/shard_map/all_gather | solution.py:110
  17.6 136.0 %collective-permute-start.6 = (f32[768,4]{0,1:T(4,128)}, f32[768,4]{0,1:T(4,128)}, u32[]{:S(2)}, u32[]{:S(2)}) collective-permute-start(f32[768,4]{0,1:T(4,128)} %param.25), channel_id=1, source_target_pairs={{0,16},{4,20},{8,24},{12,28},{16,0},{20,4},{24,8},{28,12},{1,17},{... | collective-permute-start | bytes 36872 | tf_op jit(solution)/shard_map/ppermute | solution.py:128
  80.9 71.2 %collective-permute-start.7 = (bf16[192,2048]{1,0:T(8,128)(2,1)}, bf16[192,2048]{1,0:T(8,128)(2,1)}, u32[]{:S(2)}, u32[]{:S(2)}) collective-permute-start(bf16[192,2048]{1,0:T(8,128)(2,1)} %constant_dynamic-slice_fusion.4), channel_id=1, source_target_pairs={{0,16},{4,20},{8,24},{12,28},{16,0},{20,4},{24,8},{28,12},{1,17},{... | collective-permute-start | bytes 2359304 | tf_op jit(solution)/shard_map/ppermute | solution.py:128
  181.1 75.8 %all-to-all-start = ((bf16[4,2,96,2048]{3,2,1,0:T(8,128)(2,1)}), bf16[4,2,96,2048]{3,2,1,0:T(8,128)(2,1)}, u32[]{:S(2)}, u32[]{:S(2)}) async-start(bf16[4,2,96,2048]{3,2,1,0:T(8,128)(2,1)} %pad_maximum_fusion.5), calls=%async_computation | async-start | bytes 6291456 | tf_op jit(solution)/shard_map/all_to_all | solution.py:134
  230.2 70.8 %collective-permute-start.18 = (bf16[2048,768]{0,1:T(8,128)(2,1)}, bf16[2048,768]{0,1:T(8,128)(2,1)}, u32[]{:S(2)}, u32[]{:S(2)}) collective-permute-start(bf16[2048,768]{0,1:T(8,128)(2,1)} %slice_dynamic-update-slice_fusion.26), channel_id=1, source_target_pairs={{0,2},{1,3},{2,0},{3,1},{4,6},{5,7},{6,4},{7,5},{8,10},{9,11},{10,... | collective-permute-start | bytes 9437192 | tf_op jit(solution)/shard_map/ppermute | solution.py:181
  260.9 98.0 %all-to-all-start.1 = ((bf16[8,96,2048]{2,1,0:T(8,128)(2,1)}), bf16[8,96,2048]{2,1,0:T(8,128)(2,1)}, u32[]{:S(2)}, u32[]{:S(2)}) async-start(bf16[8,96,2048]{2,1,0:T(8,128)(2,1)} %bitcast.310), calls=%async_computation.1 | async-start | bytes 6291456 | tf_op jit(solution)/shard_map/all_to_all | solution.py:245
  265.4 183.4 %all-gather.9.cloned.1.call-start = ((), (), s32[]{:S(2)}) async-start(), calls=%async_computation.9 | async-start | bytes 6488064 | tf_op jit(solution)/shard_map/all_gather | solution.py:110
  265.6 86.3 %collective-permute-start.17 = (bf16[2048,768]{0,1:T(8,128)(2,1)}, bf16[2048,768]{0,1:T(8,128)(2,1)}, u32[]{:S(2)}, u32[]{:S(2)}) collective-permute-start(bf16[2048,768]{0,1:T(8,128)(2,1)} %slice_dynamic-update-slice_fusion.26), channel_id=1, source_target_pairs={{0,1},{1,0},{2,3},{3,2},{4,5},{5,4},{6,7},{7,6},{8,9},{9,8},{10,11... | collective-permute-start | bytes 9437192 | tf_op jit(solution)/shard_map/ppermute | solution.py:177
  301.0 50.9 %collective-permute-start.19 = (bf16[2048,768]{0,1:T(8,128)(2,1)}, bf16[2048,768]{0,1:T(8,128)(2,1)}, u32[]{:S(2)}, u32[]{:S(2)}) collective-permute-start(bf16[2048,768]{0,1:T(8,128)(2,1)} %collective-permute-done.18), channel_id=1, source_target_pairs={{0,1},{1,0},{2,3},{3,2},{4,5},{5,4},{6,7},{7,6},{8,9},{9,8},{10,11... | collective-permute-start | bytes 9437192 | tf_op jit(solution)/shard_map/ppermute | solution.py:177
  304.1 39.8 %collective-permute-start.11 = (bf16[352,2048]{1,0:T(8,128)(2,1)}, bf16[352,2048]{1,0:T(8,128)(2,1)}, u32[]{:S(2)}, u32[]{:S(2)}) collective-permute-start(bf16[352,2048]{1,0:T(8,128)(2,1)} %slice_dynamic-update-slice_fusion.53), channel_id=1, source_target_pairs={{0,1},{1,0},{2,3},{3,2},{4,5},{5,4},{6,7},{7,6},{8,9},{9,8},{10,11... | collective-permute-start | bytes 4325384 | tf_op jit(solution)/shard_map/ppermute | solution.py:177
  423.1 74.0 %all-to-all-start.2 = ((bf16[8,96,2048]{2,1,0:T(8,128)(2,1)}), bf16[8,96,2048]{2,1,0:T(8,128)(2,1)}, u32[]{:S(2)}, u32[]{:S(2)}) async-start(bf16[8,96,2048]{2,1,0:T(8,128)(2,1)} %bitcast.311), calls=%async_computation.2 | async-start | bytes 6291456 | tf_op jit(solution)/shard_map/all_to_all | solution.py:245
  427.6 405.4 %reduce-scatter.8.cloned.1.call-start = ((), (), s32[]{:S(2)}) async-start(), calls=%async_computation.13 | async-start | bytes 6488064 | tf_op jit(solution)/shard_map/reduce_scatter | solution.py:116
  542.1 293.5 %reduce-scatter.6.cloned.1.call-start = ((), (), s32[]{:S(2)}) async-start(), calls=%async_computation.12 | async-start | bytes 12976128 | tf_op jit(solution)/shard_map/reduce_scatter | solution.py:116
  566.9 108.5 %collective-permute-start.42 = (bf16[2048,768]{1,0:T(8,128)(2,1)}, bf16[2048,768]{1,0:T(8,128)(2,1)}, u32[]{:S(2)}, u32[]{:S(2)}) collective-permute-start(bf16[2048,768]{1,0:T(8,128)(2,1)} %get-tuple-element.200), channel_id=1, source_target_pairs={{0,1},{1,0},{2,3},{3,2},{4,5},{5,4},{6,7},{7,6},{8,9},{9,8},{10,11... | collective-permute-start | bytes 9437192 | tf_op jit(solution)/shard_map/ppermute | solution.py:177
  582.3 77.1 %collective-permute-start.45 = (bf16[2,352,2048]{2,1,0:T(8,128)(2,1)}, bf16[2,352,2048]{2,1,0:T(8,128)(2,1)}, u32[]{:S(2)}, u32[]{:S(2)}) collective-permute-start(bf16[2,352,2048]{2,1,0:T(8,128)(2,1)} %pad_maximum_fusion.6), channel_id=1, source_target_pairs={{0,1},{1,0},{2,3},{3,2},{4,5},{5,4},{6,7},{7,6},{8,9},{9,8},{10,11... | collective-permute-start | bytes 8650760 | tf_op jit(solution)/shard_map/ppermute | solution.py:177
  600.4 75.1 %collective-permute-start.44 = (bf16[2048,768]{1,0:T(8,128)(2,1)}, bf16[2048,768]{1,0:T(8,128)(2,1)}, u32[]{:S(2)}, u32[]{:S(2)}) collective-permute-start(bf16[2048,768]{1,0:T(8,128)(2,1)} %add_convert_fusion), channel_id=1, source_target_pairs={{0,2},{1,3},{2,0},{3,1},{4,6},{5,7},{6,4},{7,5},{8,10},{9,11},{10,... | collective-permute-start | bytes 9437192 | tf_op jit(solution)/shard_map/ppermute | solution.py:181
  601.8 129.1 %all-to-all-start.3 = ((bf16[8,96,2048]{2,1,0:T(8,128)(2,1)}), bf16[8,96,2048]{2,1,0:T(8,128)(2,1)}, u32[]{:S(2)}, u32[]{:S(2)}) async-start(bf16[8,96,2048]{2,1,0:T(8,128)(2,1)} %bitcast.309), calls=%async_computation.3 | async-start | bytes 6291456 | tf_op jit(solution)/shard_map/all_to_all | solution.py:245
  606.6 269.4 %reduce-scatter.4.cloned.1.call-start = ((), (), s32[]{:S(2)}) async-start(), calls=%async_computation.11 | async-start | bytes 9437184 | tf_op jit(solution)/shard_map/reduce_scatter | solution.py:116
  658.5 67.8 %collective-permute-start.32 = (bf16[2,192,2048]{2,1,0:T(8,128)(2,1)}, bf16[2,192,2048]{2,1,0:T(8,128)(2,1)}, u32[]{:S(2)}, u32[]{:S(2)}) collective-permute-start(bf16[2,192,2048]{2,1,0:T(8,128)(2,1)} %dynamic-slice_bitcast_fusion), channel_id=1, source_target_pairs={{0,1},{1,0},{2,3},{3,2},{4,5},{5,4},{6,7},{7,6},{8,9},{9,8},{10,11... | collective-permute-start | bytes 4718600 | tf_op jit(solution)/shard_map/ppermute | solution.py:177
  663.1 39.0 %collective-permute-start.46 = (bf16[352,2048]{1,0:T(8,128)(2,1)}, bf16[352,2048]{1,0:T(8,128)(2,1)}, u32[]{:S(2)}, u32[]{:S(2)}) collective-permute-start(bf16[352,2048]{1,0:T(8,128)(2,1)} %fusion.20), channel_id=1, source_target_pairs={{0,2},{1,3},{2,0},{3,1},{4,6},{5,7},{6,4},{7,5},{8,10},{9,11},{10,... | collective-permute-start | bytes 4325384 | tf_op jit(solution)/shard_map/ppermute | solution.py:181
  761.6 46.7 %collective-permute-start.34 = (bf16[192,2048]{1,0:T(8,128)(2,1)}, bf16[192,2048]{1,0:T(8,128)(2,1)}, u32[]{:S(2)}, u32[]{:S(2)}) collective-permute-start(bf16[192,2048]{1,0:T(8,128)(2,1)} %slice_dynamic-update-slice_fusion.51), channel_id=1, source_target_pairs={{0,1},{1,0},{2,3},{3,2},{4,5},{5,4},{6,7},{7,6},{8,9},{9,8},{10,11... | collective-permute-start | bytes 2359304 | tf_op jit(solution)/shard_map/ppermute | solution.py:177
  761.6 44.2 %collective-permute-start.35 = (bf16[192,2048]{1,0:T(8,128)(2,1)}, bf16[192,2048]{1,0:T(8,128)(2,1)}, u32[]{:S(2)}, u32[]{:S(2)}) collective-permute-start(bf16[192,2048]{1,0:T(8,128)(2,1)} %slice_dynamic-update-slice_fusion.51), channel_id=1, source_target_pairs={{0,2},{1,3},{2,0},{3,1},{4,6},{5,7},{6,4},{7,5},{8,10},{9,11},{10,... | collective-permute-start | bytes 2359304 | tf_op jit(solution)/shard_map/ppermute | solution.py:181
  (135 other events, 1676.3 us)
Sparse Core Ops, SparseCore 0:
  10.1 70.7 all-gather.4
  82.3 58.8 all-gather.6
  143.3 194.9 all-gather.10
  339.7 73.9 all-gather.8
  542.2 62.2 reduce-scatter.7
  606.6 172.0 reduce-scatter.5
  781.0 94.8 reduce-scatter.3
